TPU v7x, 32 devices: a whole 2x2x4 slice. The times are simulated.
32 devices in a mesh: groups: 2 (over x), bricks: 16 (over z, y, core).
Axes of the slice: x: 2, y: 2, z: 4, core: 2. Of those that a mesh axis runs over, the one named last changes fastest.
Arguments:
- snapshots: bfloat16 [512, 32, 32, 256], P(('groups', 'bricks')), parts along dimension 0, may hold values from -30 to 30
- material: int32 [512, 1024], P(('groups', 'bricks')), parts along dimension 0, may hold values from 0 to 15
- occupancy: int32 [32, 4], P(('groups', 'bricks')), parts along dimension 0, may hold values 0 or 1
- moduli: bfloat16 [16], replicated, may hold values from 0.19921875 to 5
Outputs:
- energy_gram: float32 [512, 256], P(('groups', 'bricks')), parts along dimension 0
There are 2 independent parts, one for each index of `groups`. A program takes and returns all parts, laid end to end along the dimension named above; an argument that names none is the same for every part. Nothing has to cross between parts.
All inputs are finite; a program needn't handle non-finite values. No bound on the sum of `occupancy` on one device may be relied on, other than what follows from the above.
Results may differ from a plain program's by a relative error of at most 0.0003.
Values may be sent and summed in bfloat16 or wider, within the bound.
No kernel may reach another device: no remote copies, remote signals or barrier semaphores. Data moves between devices by JAX's collectives and lax.ppermute only.
A program may use at most 128 MiB of HBM per device.

v0:
```python
import jax
import jax.numpy as jnp
from jax import lax
from jax.sharding import PartitionSpec as P


def with_halo(block, sides, width):
    for axis, dim in sides:
        count = lax.axis_size(axis)
        forward = [(i, i + 1) for i in range(count - 1)]
        backward = [(target, source) for source, target in forward]
        low = lax.ppermute(
            lax.slice_in_dim(block, block.shape[dim] - width, None, axis=dim), axis, forward
        )
        high = lax.ppermute(lax.slice_in_dim(block, 0, width, axis=dim), axis, backward)
        block = jnp.concatenate([low, block, high], axis=dim)
    return block


def stencil(padded_field, padded_modulus):
    depth = padded_field.shape[0] - 2
    rows_y = padded_field.shape[1]
    rows_x = padded_field.shape[2]
    field_full = jnp.pad(padded_field, ((0, 0), (1, 1), (1, 1), (0, 0)))
    modulus_full = jnp.pad(padded_modulus, ((0, 0), (1, 1), (1, 1)))
    center = field_full[1 : 1 + depth, 1 : 1 + rows_y, 1 : 1 + rows_x]
    center_mod = modulus_full[1 : 1 + depth, 1 : 1 + rows_y, 1 : 1 + rows_x]
    mod_sum = jnp.zeros_like(center_mod)
    field_sum = jnp.zeros_like(center)
    product_sum = jnp.zeros_like(center)
    total_weight = 0.0
    for shift_z in (-1, 0, 1):
        for shift_y in (-1, 0, 1):
            for shift_x in (-1, 0, 1):
                nonzero = abs(shift_z) + abs(shift_y) + abs(shift_x)
                if nonzero == 0:
                    continue
                weight = (1.0, 0.5, 0.25)[nonzero - 1]
                total_weight = total_weight + weight
                near = field_full[
                    1 + shift_z : 1 + shift_z + depth,
                    1 + shift_y : 1 + shift_y + rows_y,
                    1 + shift_x : 1 + shift_x + rows_x,
                ]
                near_mod = modulus_full[
                    1 + shift_z : 1 + shift_z + depth,
                    1 + shift_y : 1 + shift_y + rows_y,
                    1 + shift_x : 1 + shift_x + rows_x,
                ]
                mod_sum = mod_sum + weight * near_mod
                field_sum = field_sum + weight * near
                product_sum = product_sum + weight * near_mod[..., None] * near
    diagonal = 0.5 * (total_weight * center_mod + mod_sum)
    return (
        diagonal[..., None] * center - 0.5 * center_mod[..., None] * field_sum - 0.5 * product_sum
    )


def local(snapshots, material, occupancy, moduli):
    depth, rows_y, rows_x, width = snapshots.shape
    owners = lax.axis_size("bricks")
    tiles = occupancy.reshape(rows_y // 16, rows_x // 16)
    occupied = jnp.repeat(jnp.repeat(tiles, 16, 0), 16, 1).astype(jnp.bfloat16)
    classes = jnp.arange(moduli.shape[0], dtype=jnp.int32)
    matches = material[..., None] == classes
    looked = jnp.sum(jnp.where(matches, moduli.astype(jnp.float32), 0.0), axis=-1)
    modulus = looked.astype(jnp.bfloat16).reshape(depth, rows_y, rows_x) * occupied[None]
    field = snapshots * occupied[None, :, :, None]
    padded_field, padded_modulus = (
        with_halo(field, (("bricks", 0),), 1),
        with_halo(modulus, (("bricks", 0),), 1),
    )
    image = stencil(padded_field.astype(jnp.float32), padded_modulus.astype(jnp.float32)).astype(
        jnp.bfloat16
    )
    field_flat = field.reshape(-1, width)
    image_flat = image.reshape(-1, width)
    scale = 1.0 / (depth * rows_y * rows_x * owners)
    own_rows = width // owners
    local_gram = lax.dot_general(
        field_flat, image_flat, (((0,), (0,)), ((), ())), preferred_element_type=jnp.float32
    )
    summed = lax.psum(local_gram, "bricks")
    start = lax.axis_index("bricks") * own_rows
    result = lax.dynamic_slice_in_dim(summed, start, own_rows, 0)
    return result * scale


def solution(mesh):
    in_specs = (
        P(("groups", "bricks"), None, None, None),
        P(("groups", "bricks"), None),
        P(("groups", "bricks"), None),
        P(),
    )
    out_specs = P(("groups", "bricks"), None)
    return jax.shard_map(local, mesh=mesh, in_specs=in_specs, out_specs=out_specs, check_vma=False)
```

profile of v0, /device:TPU:0, one launch (start us, length us, event | category | flops | bytes accessed | tf_op | source)
XLA Modules:
  0.0 343.3 jit_solution(14337007187639578546)
XLA Ops:
  6.5 0.0 all-reduce.4.cloned.1.call-start
  6.5 0.7 convert_reduce_fusion
  7.2 0.1 convert_element_type.46
  7.3 0.1 copy.10
  7.4 0.1 broadcast_in_dim.12
  7.5 0.1 convert_element_type.47
  7.6 0.1 copy.11
  7.7 0.7 convert_element_type.49
  8.3 1.1 select_reduce_fusion
  9.5 0.1 convert_element_type.51
  9.7 2.4 collective-permute-start
  12.0 1.3 collective-permute-start.1
  13.3 8.0 %broadcast_multiply_fusion = bf16[16,32,32,256]{3,2,1,0:T(8,128)(2,1)} fusion(bf16[16,32,32,256]{3,2,1,0:T(8,128)(2,1)} %param.4, bf16[32,32]{1,0:T(8,128)(2,1)S(1)} %copy.11), kind=kLoop, calls=%fused_computation.30 | loop fusion | flops 4194304 | bytes 16779264 | tf_op jit(solution)/shard_map/mul | solution.py:68
  21.4 1.3 fusion.31
  22.6 5.2 %collective-permute-start.2 = (bf16[1,32,32,256]{3,2,1,0:T(8,128)(2,1)S(1)}, bf16[1,32,32,256]{3,2,1,0:T(8,128)(2,1)S(1)}, u32[]{:S(2)}, u32[]{:S(2)}) collective-permute-start(bf16[1,32,32,256]{3,2,1,0:T(8,128)(2,1)S(1)} %get-tuple-element.5), channel_id=1, source_target_pairs={{0,1},{1,2},{2,3},{3,4},{4,5},{5,6},{6,7},{7,8},{8,9},{9,10},{10,1... | collective-permute-start | bytes 1572872 | tf_op jit(solution)/shard_map/ppermute | solution.py:12
  27.8 1.3 collective-permute-start.3
  29.1 0.0 collective-permute-done
  29.1 0.0 collective-permute-done.1
  29.2 2.3 fusion.8
  31.5 3.5 %add_multiply_fusion = (f32[16,32,32]{2,1,0:T(8,128)S(1)}, f32[16,32,32]{2,1,0:T(8,128)S(1)}, f32[16,32,32]{2,1,0:T(8,128)S(1)}, f32[16,32,32]{2,1,0:T(8,128)S(1...) fusion(f32[18,32,32]{2,1,0:T(8,128)S(1)} %maximum_convert_fusion.1), kind=kLoop, calls=%fused_computation.78 | loop fusion | flops 966656 | bytes 2129920 | tf_op jit(solution)/shard_map/mul | solution.py:53
  35.1 0.0 collective-permute-done.2
  35.1 0.0 collective-permute-done.3
  35.1 11.4 %maximum_convert_fusion = f32[18,32,32,256]{3,2,1,0:T(8,128)} fusion(bf16[1,32,32,256]{3,2,1,0:T(8,128)(2,1)S(1)} %collective-permute-done.3, bf16[16,32,32,256]{3,2,1,0:T(8,128)(2,1)} %broadcast_multiply_fusion, bf16[1,32,32,256]{3,2,1,0:T(8,128)(2,1)S(1)} %collective-permute-done.2), kind=kLoop, calls=%fused_computation.28 | loop fusion | flops 14155776 | bytes 28311552 | tf_op jit(solution)/shard_map/convert_element_type | solution.py:73
  46.4 184.7 %fusion.37 = bf16[16,32,32,256]{3,2,1,0:T(8,128)(2,1)S(1)} fusion(f32[18,32,32,256]{3,2,1,0:T(8,128)} %maximum_convert_fusion, f32[16,32,32]{2,1,0:T(8,128)} %get-tuple-element.32, f32[16,32,32]{2,1,0:T(8,128)} %get-tuple-element.31, f32[16,32,32]{2,1,0:T(8,128)} %get-tuple-element.30, f32[16,32,32]{2,1,0:T(8,128)} %get-tuple-element.29, ...), kind=kLoop, calls=%fused_computation.27.clone.clone.clone.clone.1 | loop fusion | flops 427819008 | bytes 83951616 | tf_op jit(solution)/shard_map/dot_general | solution.py:80
  231.1 6.5 %fusion.5 = f32[256,256]{1,0:T(8,128)} fusion(bf16[16,32,32,256]{3,2,1,0:T(8,128)(2,1)} %broadcast_multiply_fusion, bf16[16,32,32,256]{3,2,1,0:T(8,128)(2,1)S(1)} %fusion.37), kind=kOutput, calls=%fused_computation.31 | convolution fusion | flops 2147483648 | bytes 17039360 | tf_op jit(solution)/shard_map/dot_general | solution.py:80
  237.6 0.0 all-reduce.4.cloned.1.call-update
  237.6 97.5 %all-reduce.4.cloned.1.call-done = f32[256,256]{1,0:T(8,128)} async-done(((f32[256,256]{1,0:T(8,128)}), f32[256,256]{1,0:T(8,128)}) %all-reduce.4.cloned.1.call-update) | async-done | bytes 262160 | tf_op jit(solution)/shard_map/psum | solution.py:83
  335.1 1.3 dynamic-slice_multiply_fusion
  (4 shorter events, 0.1 us)
Async XLA Ops:
  6.5 328.6 %all-reduce.4.cloned.1.call-start = ((), (), s32[]{:S(2)}) async-start(), calls=%async_computation | async-start | bytes 524288 | tf_op jit(solution)/shard_map/psum | solution.py:83
  9.7 19.5 %collective-permute-start = (bf16[1,32,32]{2,1,0:T(8,128)(2,1)S(1)}, bf16[1,32,32]{2,1,0:T(8,128)(2,1)S(1)}, u32[]{:S(2)}, u32[]{:S(2)}) collective-permute-start(bf16[1,32,32]{2,1,0:T(8,128)(2,1)S(1)} %get-tuple-element.35), channel_id=1, source_target_pairs={{0,1},{1,2},{2,3},{3,4},{4,5},{5,6},{6,7},{7,8},{8,9},{9,10},{10,1... | collective-permute-start | bytes 6152 | tf_op jit(solution)/shard_map/ppermute | solution.py:12
  12.0 17.1 %collective-permute-start.1 = (bf16[1,32,32]{2,1,0:T(8,128)(2,1)S(1)}, bf16[1,32,32]{2,1,0:T(8,128)(2,1)S(1)}, u32[]{:S(2)}, u32[]{:S(2)}) collective-permute-start(bf16[1,32,32]{2,1,0:T(8,128)(2,1)S(1)} %get-tuple-element.36), channel_id=1, source_target_pairs={{1,0},{2,1},{3,2},{4,3},{5,4},{6,5},{7,6},{8,7},{9,8},{10,9},{11,1... | collective-permute-start | bytes 6152 | tf_op jit(solution)/shard_map/ppermute | solution.py:15
  22.6 12.4 %collective-permute-start.2 = (bf16[1,32,32,256]{3,2,1,0:T(8,128)(2,1)S(1)}, bf16[1,32,32,256]{3,2,1,0:T(8,128)(2,1)S(1)}, u32[]{:S(2)}, u32[]{:S(2)}) collective-permute-start(bf16[1,32,32,256]{3,2,1,0:T(8,128)(2,1)S(1)} %get-tuple-element.5), channel_id=1, source_target_pairs={{0,1},{1,2},{2,3},{3,4},{4,5},{5,6},{6,7},{7,8},{8,9},{9,10},{10,1... | collective-permute-start | bytes 1572872 | tf_op jit(solution)/shard_map/ppermute | solution.py:12
  27.8 7.2 %collective-permute-start.3 = (bf16[1,32,32,256]{3,2,1,0:T(8,128)(2,1)S(1)}, bf16[1,32,32,256]{3,2,1,0:T(8,128)(2,1)S(1)}, u32[]{:S(2)}, u32[]{:S(2)}) collective-permute-start(bf16[1,32,32,256]{3,2,1,0:T(8,128)(2,1)S(1)} %get-tuple-element.6), channel_id=1, source_target_pairs={{1,0},{2,1},{3,2},{4,3},{5,4},{6,5},{7,6},{8,7},{9,8},{10,9},{11,1... | collective-permute-start | bytes 1572872 | tf_op jit(solution)/shard_map/ppermute | solution.py:15
Sparse Core Ops, SparseCore 0:
  237.8 97.3 all-reduce.3
where the time goes:
time: 344 us; the launch traced here: 343 us
  other arithmetic  214 us (62%)
  waiting for transfers between devices  97.5 us (28%)
  between operations  13.5 us (4%)
  starting transfers between devices  10.1 us (3%)
  matrix products  6.48 us (2%)
    dot_general x1, other arithmetic, local(): lax.dot_general(field_flat, image_flat, (((0,), (0,)), ((), ())), preferr...  185 us
    psum x1, waiting for transfers between devices, local(): summed = lax.psum(local_gram, 'bricks')  97.5 us
    convert_element_type x1, other arithmetic, local(): padded_field.astype(jnp.float32)  11.4 us
    mul x1, other arithmetic, local(): field = snapshots * occupied[None, :, :, None]  8.04 us
    ppermute x2, starting transfers between devices, with_halo(): lax.ppermute(lax.slice_in_dim(block, block.shape[dim] - width, None, axis...  7.56 us
  transfers between devices with their start and end apart: 5, of which 1 were waited for; matrix products, arithmetic and copies ran while one was open for 4% of the time, Pallas kernels for 0%

commit v1 on v0

v1 whole, which is shorter than its diff:
```python
import jax
import jax.numpy as jnp
import numpy as np
from jax import lax
from jax.experimental import pallas as pl
from jax.experimental.pallas import tpu as pltpu
from jax.sharding import PartitionSpec as P

BLOCK = 256
EDGE = 128
F32 = jnp.float32
BF16 = jnp.bfloat16


def plane_weights(rows_x):
    source = np.arange(BLOCK + 2 * EDGE) - EDGE
    target = np.arange(BLOCK)
    step_y = np.abs(source[:, None] // rows_x - target[None, :] // rows_x)
    step_x = np.abs(source[:, None] % rows_x - target[None, :] % rows_x)
    weight = np.where(step_y == 0, 1.0, 0.5) * np.where(step_x == 0, 1.0, 0.5)
    weight = np.where((step_y <= 1) & (step_x <= 1), weight, 0.0)
    return jnp.asarray(0.5 * weight, BF16)


def lane_place(shape, rows_x):
    lane = lax.broadcasted_iota(jnp.int32, shape, 1)
    return lane // rows_x, lane % rows_x


def brick_select(occupied, rows_y, rows_x, place_y, place_x):
    o = [occupied(t).astype(F32) for t in range(4)]
    low = jnp.where(place_x < rows_x // 2, o[0], o[1])
    high = jnp.where(place_x < rows_x // 2, o[2], o[3])
    return jnp.where(place_y < rows_y // 2, low, high)


def look_up(material, moduli):
    value = jnp.zeros(material.shape, F32)
    for index in range(moduli.shape[1]):
        value = jnp.where(material == index, moduli[:, index : index + 1], value)
    return value


def smooth_plane(value, rows_y, rows_x):
    place_y, place_x = lane_place(value.shape, rows_x)
    lanes = value.shape[1]
    before = jnp.where(place_x > 0, pltpu.roll(value, 1, 1), 0.0)
    after = jnp.where(place_x < rows_x - 1, pltpu.roll(value, lanes - 1, 1), 0.0)
    value = value + 0.5 * (before + after)
    before = jnp.where(place_y > 0, pltpu.roll(value, rows_x, 1), 0.0)
    after = jnp.where(place_y < rows_y - 1, pltpu.roll(value, lanes - rows_x, 1), 0.0)
    return value + 0.5 * (before + after)


def windows(lanes):
    spans = []
    for start in range(0, lanes, BLOCK):
        low = max(start - EDGE, 0)
        high = min(start + BLOCK + EDGE, lanes)
        spans.append((start, low, high))
    return spans


def mask_weights(weights_ref, masked, occupied, rows_y, rows_x, lanes):
    for number, (start, low, high) in enumerate(windows(lanes)):
        first = low - (start - EDGE)
        shape = (high - low, BLOCK)
        voxel = lax.broadcasted_iota(jnp.int32, shape, 0) + low
        mask = brick_select(occupied, rows_y, rows_x, voxel // rows_x, voxel % rows_x)
        part = weights_ref[first : first + high - low, :].astype(F32) * mask
        masked[number, : high - low, :] = part.astype(BF16)


def pack_kernel(rows_y, rows_x, plane_ref, material_ref, occupied_ref, moduli_ref, out_ref):
    lanes = rows_y * rows_x
    occupied = lambda t: occupied_ref[0, t]
    voxel = lax.broadcasted_iota(jnp.int32, (lanes, plane_ref.shape[-1]), 0)
    mask = brick_select(occupied, rows_y, rows_x, voxel // rows_x, voxel % rows_x)
    out_ref[:lanes, :] = (plane_ref[0].astype(F32) * mask).astype(BF16)
    place_y, place_x = lane_place((8, lanes), rows_x)
    value = look_up(material_ref[...], moduli_ref[...].astype(F32))
    value = value * brick_select(occupied, rows_y, rows_x, place_y, place_x)
    width = out_ref.shape[1]
    for part in range(lanes // width):
        row = value[0:1, part * width : (part + 1) * width]
        start = lanes + 16 * part
        out_ref[start : start + 16, :] = jnp.broadcast_to(row, (16, width)).astype(BF16)


def image_block(ft, smooth, m8, c8, spread):
    rows, lanes = ft.shape
    shape = (rows // 8, 8, lanes)
    field = ft.astype(F32).reshape(shape)
    out = c8[None] * field - m8[None] * smooth.reshape(shape)
    return out.reshape(rows, lanes).astype(BF16)


def main_kernel(
    rows_y, rows_x,
    snapshots_ref, material_ref, occupied_ref, moduli_ref, weights_ref,
    out_ref,
    field, ft, last, pair, image, masked, m8, c8, sems,
):
    depth, lanes, width = snapshots_ref.shape
    occupied = lambda t: occupied_ref[0, t]

    def copy(z):
        return pltpu.make_async_copy(snapshots_ref.at[z], field.at[z], sems.at[z])

    for z in range(depth):
        copy(z).start()

    shape = (depth, lanes)
    place_y, place_x = lane_place(shape, rows_x)
    mask = brick_select(occupied, rows_y, rows_x, place_y, place_x)
    modulus = look_up(material_ref[...], moduli_ref[...].astype(F32)) * mask
    smooth = smooth_plane(modulus, rows_y, rows_x)
    place_z = lax.broadcasted_iota(jnp.int32, shape, 0)
    before = jnp.where(place_z > 0, pltpu.roll(smooth, 1, 0), 0.0)
    after = jnp.where(place_z < depth - 1, pltpu.roll(smooth, depth - 1, 0), 0.0)
    smooth = smooth + 0.5 * (before + after)
    center = (4.0 * modulus + 0.5 * smooth) * mask
    for z in range(depth):
        m8[z] = jnp.broadcast_to(modulus[z : z + 1], (8, lanes))
        c8[z] = jnp.broadcast_to(center[z : z + 1], (8, lanes))
    mask_weights(weights_ref, masked, occupied, rows_y, rows_x, lanes)

    spans = windows(lanes)
    out_ref[...] = jnp.zeros_like(out_ref)

    def smoothed(number, slot):
        start, low, high = spans[number]
        return jnp.dot(
            ft[slot, :, low:high], masked[number, : high - low, :], preferred_element_type=F32
        )

    def emit(z, slot, number, both):
        block = pl.ds(spans[number][0], BLOCK)
        image[:, block] = image_block(
            ft[slot, :, block], both, m8[z, :, block], c8[z, :, block], None
        )

    def gram(z):
        out_ref[...] += jnp.dot(image[...], field[z], preferred_element_type=F32)

    copy(0).wait()
    ft[0] = field[0].T
    for number in range(len(spans)):
        block = pl.ds(spans[number][0], BLOCK)
        new = smoothed(number, 0)
        last[:, block] = new
        pair[:, block] = new

    def step(z, slot):
        copy(z).wait()
        ft[slot] = field[z].T
        for number in range(len(spans)):
            block = pl.ds(spans[number][0], BLOCK)
            new = smoothed(number, slot)
            now = last[:, block] + new
            emit(z - 1, 1 - slot, number, pair[:, block] + now)
            last[:, block] = new
            pair[:, block] = now
        gram(z - 1)

    def two(index, carry):
        z = 2 * index + 1
        step(z, 1)
        step(z + 1, 0)
        return carry

    lax.fori_loop(0, (depth - 2) // 2, two, 0)
    step(depth - 1, 1)
    for number in range(len(spans)):
        block = pl.ds(spans[number][0], BLOCK)
        emit(depth - 1, 1, number, pair[:, block] + last[:, block])
    gram(depth - 1)


def edge_kernel(
    rows_y, rows_x, scale,
    snapshots_ref, halo_ref, material_ref, occupied_ref, moduli_ref, weights_ref, gram_ref,
    out_ref,
    own, masked, image, sem,
):
    depth, lanes, width = snapshots_ref.shape
    occupied = lambda t: occupied_ref[0, t]
    load = pltpu.make_async_copy(snapshots_ref.at[depth - 1], own, sem)
    load.start()
    shape = (8, lanes)
    place_y, place_x = lane_place(shape, rows_x)
    mask = brick_select(occupied, rows_y, rows_x, place_y, place_x)
    value = look_up(material_ref[depth - 8 :, :], moduli_ref[...].astype(F32))
    own_mod = jnp.broadcast_to(value[7:8], shape) * mask
    rows = [
        halo_ref[lanes + 16 * part : lanes + 16 * part + 16, :].astype(F32)[:8]
        for part in range(lanes // width)
    ]
    halo_mod = jnp.concatenate(rows, axis=1)
    own_c = 0.25 * smooth_plane(halo_mod, rows_y, rows_x) * mask
    halo_c = 0.25 * smooth_plane(own_mod, rows_y, rows_x)
    mask_weights(weights_ref, masked, occupied, rows_y, rows_x, lanes)
    halo_t = halo_ref[:lanes, :].T
    load.wait()
    own_t = own[...].T
    for number, (start, low, high) in enumerate(windows(lanes)):
        block = slice(start, start + BLOCK)
        first = low - (start - EDGE)
        from_halo = jnp.dot(
            halo_t[:, low:high], weights_ref[first : first + high - low, :],
            preferred_element_type=F32,
        )
        from_own = jnp.dot(
            own_t[:, low:high], masked[number, : high - low, :], preferred_element_type=F32
        )
        image[0, :, block] = image_block(
            own_t[:, block], from_halo, own_mod[:, block], own_c[:, block], None
        )
        image[1, :, block] = image_block(
            halo_t[:, block], from_own, halo_mod[:, block], halo_c[:, block], None
        )
    total = gram_ref[...]
    total += jnp.dot(image[0], own[...], preferred_element_type=F32)
    total += jnp.dot(image[1], halo_ref[:lanes, :], preferred_element_type=F32)
    out_ref[...] = (total + total.T) * scale


def scatter_sum(value, axis):
    count = lax.axis_size(axis)
    position = lax.axis_index(axis)
    own = value.shape[0] // count
    step = 1
    while step < count:
        value = value.reshape(-1, 2, own, value.shape[-1])
        side = (position // step) % 2
        keep = lax.dynamic_index_in_dim(value, side, 1, keepdims=False)
        give = lax.dynamic_index_in_dim(value, 1 - side, 1, keepdims=False)
        swap = [(device, device ^ step) for device in range(count)]
        value = keep + lax.ppermute(give, axis, swap)
        step *= 2
    return value.reshape(own, value.shape[-1])


def local(snapshots, material, occupancy, moduli):
    depth, rows_y, rows_x, width = snapshots.shape
    lanes = rows_y * rows_x
    owners = lax.axis_size("bricks")
    scale = 1.0 / (depth * lanes * owners)
    planes = snapshots.reshape(depth, lanes, width)
    moduli = moduli.reshape(1, -1)
    weights = plane_weights(rows_x)
    vmem = pl.BlockSpec(memory_space=pltpu.VMEM)
    smem = pl.BlockSpec(memory_space=pltpu.SMEM)
    hbm = pl.BlockSpec(memory_space=pl.ANY)
    spans = len(windows(lanes))
    packed_rows = lanes + 16 * (lanes // width)

    packed = pl.pallas_call(
        lambda *refs: pack_kernel(rows_y, rows_x, *refs),
        grid=(1,),
        in_specs=[
            pl.BlockSpec((1, lanes, width), lambda i: (0, 0, 0)),
            pl.BlockSpec((8, lanes), lambda i: (0, 0)),
            smem,
            pl.BlockSpec(moduli.shape, lambda i: (0, 0)),
        ],
        out_specs=pl.BlockSpec((packed_rows, width), lambda i: (0, 0)),
        out_shape=jax.ShapeDtypeStruct((packed_rows, width), BF16),
        name="pack",
    )(planes, material, occupancy, moduli)

    halo = lax.ppermute(packed, "bricks", [(i + 1, i) for i in range(owners - 1)])

    gram = pl.pallas_call(
        lambda *refs: main_kernel(rows_y, rows_x, *refs),
        in_specs=[hbm, vmem, smem, vmem, vmem],
        out_specs=vmem,
        out_shape=jax.ShapeDtypeStruct((width, width), F32),
        scratch_shapes=[
            pltpu.VMEM((depth, lanes, width), BF16),
            pltpu.VMEM((2, width, lanes), BF16),
            pltpu.VMEM((width, lanes), F32),
            pltpu.VMEM((width, lanes), F32),
            pltpu.VMEM((width, lanes), BF16),
            pltpu.VMEM((spans, BLOCK + 2 * EDGE, BLOCK), BF16),
            pltpu.VMEM((depth, 8, lanes), F32),
            pltpu.VMEM((depth, 8, lanes), F32),
            pltpu.SemaphoreType.DMA((depth,)),
        ],
        compiler_params=pltpu.CompilerParams(vmem_limit_bytes=40 << 20),
        cost_estimate=pl.CostEstimate(
            flops=6 * depth * lanes * width * width,
            bytes_accessed=2 * depth * lanes * width,
            transcendentals=0,
        ),
        name="interior",
    )(planes, material, occupancy, moduli, weights)

    share = pl.pallas_call(
        lambda *refs: edge_kernel(rows_y, rows_x, scale, *refs),
        in_specs=[hbm, vmem, vmem, smem, vmem, vmem, vmem],
        out_specs=vmem,
        out_shape=jax.ShapeDtypeStruct((width, width), F32),
        scratch_shapes=[
            pltpu.VMEM((lanes, width), BF16),
            pltpu.VMEM((spans, BLOCK + 2 * EDGE, BLOCK), BF16),
            pltpu.VMEM((2, width, lanes), BF16),
            pltpu.SemaphoreType.DMA(()),
        ],
        compiler_params=pltpu.CompilerParams(vmem_limit_bytes=32 << 20),
        cost_estimate=pl.CostEstimate(
            flops=12 * lanes * width * width, bytes_accessed=4 * lanes * width, transcendentals=0
        ),
        name="edge",
    )(planes, halo, material, occupancy, moduli, weights, gram)
    return scatter_sum(share, "bricks")


def solution(mesh):
    in_specs = (
        P(("groups", "bricks"), None, None, None),
        P(("groups", "bricks"), None),
        P(("groups", "bricks"), None),
        P(),
    )
    out_specs = P(("groups", "bricks"), None)
    return jax.shard_map(local, mesh=mesh, in_specs=in_specs, out_specs=out_specs, check_vma=False)
```

time: 344 us -> 40.2 us (0.12)
  other arithmetic: 214 us -> 0.64 us
  waiting for transfers between devices: 97.5 us -> 7.21 us
  Pallas kernels: 0 us -> 17.5 us
  between operations: 13.5 us -> 0.14 us
  matrix products: 6.48 us -> 0 us
    dot_general x1 -> x0, other arithmetic: 185 us -> none  [local(): lax.dot_general(field_flat, image_flat, (((0,), (0,)), ((), ())), preferr...]
    psum x1 -> x0, waiting for transfers between devices: 97.5 us -> none  [local(): summed = lax.psum(local_gram, 'bricks')]
    pallas_call x0 -> x3, Pallas kernels: none -> 17.5 us  [the longest x1 13.1 us: local(): pl.pallas_call(lambda *refs: main_kernel(rows_y, rows_x, *refs), in_specs...]
    mul x5 -> x0, other arithmetic: 15.2 us -> none  [the longest x1 8.04 us: local(): field = snapshots * occupied[None, :, :, None]]
    convert_element_type x4 -> x0, other arithmetic: 12.7 us -> none  [the longest x1 11.4 us: local(): padded_field.astype(jnp.float32)]
    ppermute x4 -> x5, waiting for transfers between devices: 0.01 us -> 7.21 us  [the longest x4 7.2 us: scatter_sum(): value = keep + lax.ppermute(give, axis, swap)]
    dot_general x1 -> x0, matrix products: 6.48 us -> none  [local(): lax.dot_general(field_flat, image_flat, (((0,), (0,)), ((), ())), preferr...]
    ppermute x4 -> x5, starting transfers between devices: 10.1 us -> 11.1 us  [the longest x4 9.81 us: scatter_sum(): value = keep + lax.ppermute(give, axis, swap)]
  transfers between devices with their start and end apart: 5 -> 5, of which waited for: 1 -> 4; matrix products, arithmetic and copies ran while one was open for 4% -> 0% of each run, Pallas kernels for 0% -> 33%
where the time goes in v1:
time: 40.2 us; the launch traced here: 40 us
  Pallas kernels  17.5 us (44%)
  starting transfers between devices  11.1 us (28%)
  waiting for transfers between devices  7.21 us (18%)
  local copies, waits for them, and re-layouts  3.44 us (9%)
  other arithmetic  0.64 us (2%)
    pallas_call x1, Pallas kernels, local(): pl.pallas_call(lambda *refs: main_kernel(rows_y, rows_x, *refs), in_specs...  13.1 us
    ppermute x4, starting transfers between devices, scatter_sum(): value = keep + lax.ppermute(give, axis, swap)  9.81 us
    ppermute x4, waiting for transfers between devices, scatter_sum(): value = keep + lax.ppermute(give, axis, swap)  7.2 us
    unnamed x12, local copies, waits for them, and re-layouts  3.4 us
    pallas_call x1, Pallas kernels, local(): pl.pallas_call(lambda *refs: edge_kernel(rows_y, rows_x, scale, *refs), i...  2.22 us
    pallas_call x1, Pallas kernels, local(): pl.pallas_call(lambda *refs: pack_kernel(rows_y, rows_x, *refs), grid=(1,...  2.2 us
    ppermute x1, starting transfers between devices, local(): lax.ppermute(packed, 'bricks', [(i + 1, i) for i in range(owners - 1)])  1.28 us
  transfers between devices with their start and end apart: 5, of which 4 were waited for; matrix products, arithmetic and copies ran while one was open for 0% of the time, Pallas kernels for 33%

profile of v1, /device:TPU:0, one launch (start us, length us, event | category | flops | bytes accessed | tf_op | source)
XLA Modules:
  0.0 40.0 jit_solution(7330773697763876139)
XLA Ops:
  0.0 0.0 copy-start.3
  0.0 0.0 copy-start.2
  0.0 0.0 copy-start.4
  0.0 0.0 copy-start.5
  0.0 2.2 %pack.1 = bf16[1088,256]{1,0:T(8,128)(2,1)} custom-call(bf16[16,1024,256]{2,1,0:T(8,128)(2,1)} %bitcast.19, s32[16,1024]{1,0:T(8,128)} %refs_2_.5, s32[1,4]{1,0:T(1,128)} %refs_3_.1, bf16[1,16]{1,0:T(2,128)(2,1)} %bitcast.24), custom_call_target="tpu_custom_call" | custom-call | tf_op jit(solution)/shard_map/pack/pallas_call | solution.py:258
  2.2 1.3 %collective-permute-start = (bf16[1088,256]{1,0:T(8,128)(2,1)}, bf16[1088,256]{1,0:T(8,128)(2,1)S(1)}, u32[]{:S(2)}, u32[]{:S(2)}) collective-permute-start(bf16[1088,256]{1,0:T(8,128)(2,1)} %pack.1), channel_id=1, source_target_pairs={{1,0},{2,1},{3,2},{4,3},{5,4},{6,5},{7,6},{8,7},{9,8},{10,9},{11,1... | collective-permute-start | bytes 1671176 | tf_op jit(solution)/shard_map/ppermute | solution.py:272
  3.5 0.0 copy-done.3
  3.5 0.0 copy-done.2
  3.5 0.0 copy-done.4
  3.6 0.0 copy-done.5
  3.6 0.0 copy-start
  3.6 3.4 %copy-done = bf16[16,32,32,256]{3,2,1,0:T(8,128)(2,1)S(1)} copy-done((bf16[16,32,32,256]{3,2,1,0:T(8,128)(2,1)S(1)}, bf16[16,32,32,256]{3,2,1,0:T(8,128)(2,1)}, u32[]{:S(2)}) %copy-start) | copy-done | bytes 8388632
  6.9 0.0 copy-start.1
  6.9 13.1 %interior.1.refs_6_ = f32[256,256]{1,0:T(8,128)S(1)} custom-call(bf16[16,1024,256]{2,1,0:T(8,128)(2,1)S(1)} %bitcast.20, s32[16,1024]{1,0:T(8,128)S(1)} %copy-done.2, s32[1,4]{1,0:T(1,128)S(1)} %copy-done.4, bf16[1,16]{1,0:T(2,128)(2,1)S(1)} %bitcast.25, bf16[512,256]{1,0:T(8,128)(2,1)S(1)} %copy-done.3), custom_call_target="tpu_custom_call" | custom-call | flops 6442450944 | bytes 8388608 | tf_op jit(solution)/shard_map/interior/pallas_call | solution.py:274
  20.0 0.0 collective-permute-done.refs_1_
  20.0 0.0 copy-done.1
  20.0 2.2 %edge.1 = f32[256,256]{1,0:T(8,128)S(1)} custom-call(bf16[16,1024,256]{2,1,0:T(8,128)(2,1)S(1)} %bitcast.21, bf16[1088,256]{1,0:T(8,128)(2,1)S(1)} %collective-permute-done.refs_1_, s32[16,1024]{1,0:T(8,128)S(1)} %copy-done.2, s32[1,4]{1,0:T(1,128)S(1)} %copy-done.4, bf16[1,16]{1,0:T(2,128)(2,1)S(1)} %bitcast.26, bf16[512,256]{1,0:T(8,128)(2,1)S(1)} %copy-done.3, ...), custom_call_target="tpu_custom_call" | custom-call | flops 805306368 | bytes 1048576 | tf_op jit(solution)/shard_map/edge/pallas_call | solution.py:299
  22.3 1.2 %collective-permute-start.1 = (f32[8,16,256]{2,1,0:T(8,128)S(1)}, f32[8,16,256]{2,1,0:T(8,128)S(1)}, u32[]{:S(2)}, u32[]{:S(2)}) collective-permute-start(f32[8,16,256]{2,1,0:T(8,128)S(1)} %dynamic-slice_bitcast_fusion), channel_id=1, source_target_pairs={{0,1},{1,0},{2,3},{3,2},{4,5},{5,4},{6,7},{7,6},{8,9},{9,8},{10,11... | collective-permute-start | bytes 393224 | tf_op jit(solution)/shard_map/ppermute | solution.py:239
  23.5 1.0 %collective-permute-done.1 = f32[8,16,256]{2,1,0:T(8,128)S(1)} collective-permute-done((f32[8,16,256]{2,1,0:T(8,128)S(1)}, f32[8,16,256]{2,1,0:T(8,128)S(1)}, u32[]{:S(2)}, u32[]{:S(2)}) %collective-permute-start.1) | collective-permute-done | bytes 131104 | tf_op jit(solution)/shard_map/ppermute | solution.py:239
  24.5 3.1 %collective-permute-start.2 = (f32[4,16,256]{2,1,0:T(8,128)S(1)}, f32[4,16,256]{2,1,0:T(8,128)S(1)}, u32[]{:S(2)}, u32[]{:S(2)}) collective-permute-start(f32[4,16,256]{2,1,0:T(8,128)S(1)} %dynamic-slice_bitcast_fusion.1), channel_id=1, source_target_pairs={{0,2},{1,3},{2,0},{3,1},{4,6},{5,7},{6,4},{7,5},{8,10},{9,11},{10,... | collective-permute-start | bytes 196616 | tf_op jit(solution)/shard_map/ppermute | solution.py:239
  27.6 2.6 %collective-permute-done.2 = f32[4,16,256]{2,1,0:T(8,128)S(1)} collective-permute-done((f32[4,16,256]{2,1,0:T(8,128)S(1)}, f32[4,16,256]{2,1,0:T(8,128)S(1)}, u32[]{:S(2)}, u32[]{:S(2)}) %collective-permute-start.2) | collective-permute-done | bytes 65568 | tf_op jit(solution)/shard_map/ppermute | solution.py:239
  30.2 2.5 %collective-permute-start.3 = (f32[2,16,256]{2,1,0:T(8,128)S(1)}, f32[2,16,256]{2,1,0:T(8,128)S(1)}, u32[]{:S(2)}, u32[]{:S(2)}) collective-permute-start(f32[2,16,256]{2,1,0:T(8,128)S(1)} %dynamic-slice_bitcast_fusion.2), channel_id=1, source_target_pairs={{0,4},{1,5},{2,6},{3,7},{4,0},{5,1},{6,2},{7,3},{8,12},{9,13},{10,... | collective-permute-start | bytes 98312 | tf_op jit(solution)/shard_map/ppermute | solution.py:239
  32.7 1.9 %collective-permute-done.3 = f32[2,16,256]{2,1,0:T(8,128)S(1)} collective-permute-done((f32[2,16,256]{2,1,0:T(8,128)S(1)}, f32[2,16,256]{2,1,0:T(8,128)S(1)}, u32[]{:S(2)}, u32[]{:S(2)}) %collective-permute-start.3) | collective-permute-done | bytes 32800 | tf_op jit(solution)/shard_map/ppermute | solution.py:239
  34.6 3.1 %collective-permute-start.4 = (f32[1,16,256]{2,1,0:T(8,128)S(1)}, f32[1,16,256]{2,1,0:T(8,128)S(1)}, u32[]{:S(2)}, u32[]{:S(2)}) collective-permute-start(f32[1,16,256]{2,1,0:T(8,128)S(1)} %constant_dynamic-slice_fusion), channel_id=1, source_target_pairs={{0,8},{1,9},{2,10},{3,11},{4,12},{5,13},{6,14},{7,15},{8,0},{9,1},... | collective-permute-start | bytes 49160 | tf_op jit(solution)/shard_map/ppermute | solution.py:239
  37.7 1.7 %collective-permute-done.4 = f32[1,16,256]{2,1,0:T(8,128)S(1)} collective-permute-done((f32[1,16,256]{2,1,0:T(8,128)S(1)}, f32[1,16,256]{2,1,0:T(8,128)S(1)}, u32[]{:S(2)}, u32[]{:S(2)}) %collective-permute-start.4) | collective-permute-done | bytes 16416 | tf_op jit(solution)/shard_map/ppermute | solution.py:239
  39.4 0.6 %add_bitcast_fusion = f32[16,256]{1,0:T(8,128)} fusion(f32[1,16,256]{2,1,0:T(8,128)S(1)} %collective-permute-done.4, f32[2,16,256]{2,1,0:T(8,128)S(1)} %bitcast_add_fusion.2, s32[]{:T(128)S(6)} %select_n.71), kind=kLoop, calls=%fused_computation.6 | loop fusion | flops 4096 | bytes 49156 | tf_op jit(solution)/shard_map/reshape | solution.py:241
  (7 shorter events, 0.1 us)
Async XLA Ops:
  0.0 3.5 %copy-start.3 = (bf16[512,256]{1,0:T(8,128)(2,1)S(1)}, bf16[512,256]{1,0:T(8,128)(2,1)}, u32[]{:S(2)}) copy-start(bf16[512,256]{1,0:T(8,128)(2,1)} %constant.99.clone.refs_4_.refs_5_) | copy-start | bytes 786436
  0.0 3.5 %copy-start.2 = (s32[16,1024]{1,0:T(8,128)S(1)}, s32[16,1024]{1,0:T(8,128)}, u32[]{:S(2)}) copy-start(s32[16,1024]{1,0:T(8,128)} %refs_2_.5) | copy-start | bytes 196612
  0.0 3.5 %copy-start.4 = (s32[1,4]{1,0:T(1,128)S(1)}, s32[1,4]{1,0:T(1,128)}, u32[]{:S(2)}) copy-start(s32[1,4]{1,0:T(1,128)} %refs_3_.1) | copy-start | bytes 52
  0.0 3.5 %copy-start.5 = (bf16[16]{0:T(256)(128)(2,1)S(1)}, bf16[16]{0:T(256)(128)(2,1)}, u32[]{:S(2)}) copy-start(bf16[16]{0:T(256)(128)(2,1)} %param.8) | copy-start | bytes 100
  2.2 17.8 %collective-permute-start = (bf16[1088,256]{1,0:T(8,128)(2,1)}, bf16[1088,256]{1,0:T(8,128)(2,1)S(1)}, u32[]{:S(2)}, u32[]{:S(2)}) collective-permute-start(bf16[1088,256]{1,0:T(8,128)(2,1)} %pack.1), channel_id=1, source_target_pairs={{1,0},{2,1},{3,2},{4,3},{5,4},{6,5},{7,6},{8,7},{9,8},{10,9},{11,1... | collective-permute-start | bytes 1671176 | tf_op jit(solution)/shard_map/ppermute | solution.py:272
  3.6 3.4 %copy-start = (bf16[16,32,32,256]{3,2,1,0:T(8,128)(2,1)S(1)}, bf16[16,32,32,256]{3,2,1,0:T(8,128)(2,1)}, u32[]{:S(2)}) copy-start(bf16[16,32,32,256]{3,2,1,0:T(8,128)(2,1)} %param.5) | copy-start | bytes 25165828
  6.9 13.1 %copy-start.1 = (bf16[16,32,32,256]{3,2,1,0:T(8,128)(2,1)S(1)}, bf16[16,32,32,256]{3,2,1,0:T(8,128)(2,1)}, u32[]{:S(2)}) copy-start(bf16[16,32,32,256]{3,2,1,0:T(8,128)(2,1)} %param.5) | copy-start | bytes 25165828
  22.3 2.2 %collective-permute-start.1 = (f32[8,16,256]{2,1,0:T(8,128)S(1)}, f32[8,16,256]{2,1,0:T(8,128)S(1)}, u32[]{:S(2)}, u32[]{:S(2)}) collective-permute-start(f32[8,16,256]{2,1,0:T(8,128)S(1)} %dynamic-slice_bitcast_fusion), channel_id=1, source_target_pairs={{0,1},{1,0},{2,3},{3,2},{4,5},{5,4},{6,7},{7,6},{8,9},{9,8},{10,11... | collective-permute-start | bytes 393224 | tf_op jit(solution)/shard_map/ppermute | solution.py:239
  24.5 5.7 %collective-permute-start.2 = (f32[4,16,256]{2,1,0:T(8,128)S(1)}, f32[4,16,256]{2,1,0:T(8,128)S(1)}, u32[]{:S(2)}, u32[]{:S(2)}) collective-permute-start(f32[4,16,256]{2,1,0:T(8,128)S(1)} %dynamic-slice_bitcast_fusion.1), channel_id=1, source_target_pairs={{0,2},{1,3},{2,0},{3,1},{4,6},{5,7},{6,4},{7,5},{8,10},{9,11},{10,... | collective-permute-start | bytes 196616 | tf_op jit(solution)/shard_map/ppermute | solution.py:239
  30.2 4.4 %collective-permute-start.3 = (f32[2,16,256]{2,1,0:T(8,128)S(1)}, f32[2,16,256]{2,1,0:T(8,128)S(1)}, u32[]{:S(2)}, u32[]{:S(2)}) collective-permute-start(f32[2,16,256]{2,1,0:T(8,128)S(1)} %dynamic-slice_bitcast_fusion.2), channel_id=1, source_target_pairs={{0,4},{1,5},{2,6},{3,7},{4,0},{5,1},{6,2},{7,3},{8,12},{9,13},{10,... | collective-permute-start | bytes 98312 | tf_op jit(solution)/shard_map/ppermute | solution.py:239
  34.6 4.8 %collective-permute-start.4 = (f32[1,16,256]{2,1,0:T(8,128)S(1)}, f32[1,16,256]{2,1,0:T(8,128)S(1)}, u32[]{:S(2)}, u32[]{:S(2)}) collective-permute-start(f32[1,16,256]{2,1,0:T(8,128)S(1)} %constant_dynamic-slice_fusion), channel_id=1, source_target_pairs={{0,8},{1,9},{2,10},{3,11},{4,12},{5,13},{6,14},{7,15},{8,0},{9,1},... | collective-permute-start | bytes 49160 | tf_op jit(solution)/shard_map/ppermute | solution.py:239

commit v2 on v1

v2 whole, which is shorter than its diff:
```python
import jax
import jax.numpy as jnp
import numpy as np
from jax import lax
from jax.experimental import pallas as pl
from jax.experimental.pallas import tpu as pltpu
from jax.sharding import PartitionSpec as P

BLOCK = 256
EDGE = 128
F32 = jnp.float32
BF16 = jnp.bfloat16


def plane_weights(rows_x):
    source = np.arange(BLOCK + 2 * EDGE) - EDGE
    target = np.arange(BLOCK)
    step_y = np.abs(source[:, None] // rows_x - target[None, :] // rows_x)
    step_x = np.abs(source[:, None] % rows_x - target[None, :] % rows_x)
    weight = np.where(step_y == 0, 1.0, 0.5) * np.where(step_x == 0, 1.0, 0.5)
    weight = np.where((step_y <= 1) & (step_x <= 1), weight, 0.0)
    return jnp.asarray(0.5 * weight, BF16)


def lane_place(shape, rows_x):
    lane = lax.broadcasted_iota(jnp.int32, shape, 1)
    return lane // rows_x, lane % rows_x


def brick_select(occupied, rows_y, rows_x, place_y, place_x):
    o = [occupied(t).astype(F32) for t in range(4)]
    low = jnp.where(place_x < rows_x // 2, o[0], o[1])
    high = jnp.where(place_x < rows_x // 2, o[2], o[3])
    return jnp.where(place_y < rows_y // 2, low, high)


def look_up(material, moduli):
    value = jnp.zeros(material.shape, F32)
    for index in range(moduli.shape[1]):
        value = jnp.where(material == index, moduli[:, index : index + 1], value)
    return value


def smooth_plane(value, rows_y, rows_x):
    place_y, place_x = lane_place(value.shape, rows_x)
    lanes = value.shape[1]
    before = jnp.where(place_x > 0, pltpu.roll(value, 1, 1), 0.0)
    after = jnp.where(place_x < rows_x - 1, pltpu.roll(value, lanes - 1, 1), 0.0)
    value = value + 0.5 * (before + after)
    before = jnp.where(place_y > 0, pltpu.roll(value, rows_x, 1), 0.0)
    after = jnp.where(place_y < rows_y - 1, pltpu.roll(value, lanes - rows_x, 1), 0.0)
    return value + 0.5 * (before + after)


def windows(lanes):
    spans = []
    for start in range(0, lanes, BLOCK):
        low = max(start - EDGE, 0)
        high = min(start + BLOCK + EDGE, lanes)
        spans.append((start, low, high))
    return spans


def pack_kernel(
    rows_y, rows_x, snapshots_ref, material_ref, occupied_ref, moduli_ref, out_ref, rows, packed, sems
):
    lanes, width = snapshots_ref.shape[1:]
    plane = pltpu.make_async_copy(snapshots_ref.at[0], out_ref.at[pl.ds(0, lanes)], sems.at[0])
    plane.start()
    occupied = lambda t: occupied_ref[0, t]
    place_y, place_x = lane_place((8, lanes), rows_x)
    value = look_up(material_ref[:8, :], moduli_ref[...].astype(F32))
    value = value * brick_select(occupied, rows_y, rows_x, place_y, place_x)
    rows[...] = jnp.zeros_like(rows)
    for part in range(lanes // width):
        rows[part : part + 1, :] = value[0:1, part * width : (part + 1) * width]
    packed[...] = rows[...].astype(BF16)
    extra = pltpu.make_async_copy(packed, out_ref.at[pl.ds(lanes, 16)], sems.at[1])
    extra.start()
    plane.wait()
    extra.wait()


def main_kernel(
    rows_y, rows_x,
    snapshots_ref, material_ref, occupied_ref, moduli_ref, weights_ref,
    out_ref,
    field, lhs, last, pair, image, modulus_rows, center_columns, masked, sems,
):
    depth, lanes, width = snapshots_ref.shape
    blocks = lanes // BLOCK
    per_block = BLOCK // rows_x
    reach = BLOCK + 2 * rows_x
    occupied = lambda t: occupied_ref[0, t]

    def copy(z):
        return pltpu.make_async_copy(snapshots_ref.at[z], field.at[z], sems.at[z])

    for z in range(depth):
        copy(z).start()

    shape = (depth, lanes)
    place_y, place_x = lane_place(shape, rows_x)
    mask = brick_select(occupied, rows_y, rows_x, place_y, place_x)
    modulus = look_up(material_ref[...], moduli_ref[...].astype(F32)) * mask
    smooth = smooth_plane(modulus, rows_y, rows_x)
    place_z = lax.broadcasted_iota(jnp.int32, shape, 0)
    before = jnp.where(place_z > 0, pltpu.roll(smooth, 1, 0), 0.0)
    after = jnp.where(place_z < depth - 1, pltpu.roll(smooth, depth - 1, 0), 0.0)
    smooth = smooth + 0.5 * (before + after)
    center = (4.0 * modulus + 0.5 * smooth) * mask
    for z in range(depth):
        modulus_rows[z] = jnp.broadcast_to(modulus[z : z + 1], (16, lanes)).astype(BF16)
    center_columns[...] = jnp.concatenate([center, jnp.zeros((128 - depth, lanes), F32)], 0).T
    lhs[...] = jnp.zeros_like(lhs)
    on = [occupied(t) > 0 for t in range(4)]
    for block in range(blocks):
        for row in range(0, reach, 16):
            voxel = min(max(block * BLOCK - rows_x + row, 0), lanes - 16)
            brick = voxel // rows_x // (rows_y // 2) * 2 + voxel % rows_x // (rows_x // 2)
            part = weights_ref[EDGE - rows_x + row : EDGE - rows_x + row + 16, :]
            masked[block, row : row + 16, :] = jnp.where(on[brick], part, jnp.zeros_like(part))
    out_ref[...] = jnp.zeros_like(out_ref)

    half = BLOCK // 2
    span = half + 2 * rows_x

    def smoothed(z, block):
        slot = (z * blocks + block) % 2
        scale = modulus_rows[z, :, block * BLOCK : (block + 1) * BLOCK]
        for side in range(2):
            rows = slice(side * (reach - span), side * (reach - span) + span)
            columns = slice(side * half, (side + 1) * half)
            part = masked[block, rows, columns].reshape(span // 16, 16, half)
            lhs[slot, rows, columns] = (part * scale[None, :, columns]).reshape(span, half)
        return jnp.dot(
            lhs[slot], field[z, block * BLOCK : (block + 1) * BLOCK, :],
            preferred_element_type=F32,
        )

    def plane(z, sink):
        above, below = None, None
        for block in range(blocks):
            value = smoothed(z, block)
            own = [value[rows_x * (i + 1) : rows_x * (i + 2)] for i in range(per_block)]
            if block > 0:
                sink(z, per_block * block - 1, above + value[:rows_x])
                own[0] = own[0] + below
            for i in range(per_block - 1):
                sink(z, per_block * block + i, own[i])
            above, below = own[-1], value[rows_x * (per_block + 1) :]
        sink(z, per_block * blocks - 1, above)

    def start(z, y, new):
        rows = pl.ds(y * rows_x, rows_x)
        last[rows, :] = new
        pair[rows, :] = new

    def emit(z, y, new):
        rows = pl.ds(y * rows_x, rows_x)
        now = last[rows, :] if new is None else last[rows, :] + new
        both = pair[rows, :] + now
        scale = jnp.broadcast_to(center_columns[rows, z - 1 : z], (rows_x, width))
        value = scale * field[z - 1, rows, :].astype(F32) - both
        image[(z - 1) % 2, rows, :] = value.astype(BF16)
        if new is not None:
            last[rows, :] = new
            pair[rows, :] = now

    def gram(z):
        out_ref[...] += jnp.dot(image[z % 2].T, field[z], preferred_element_type=F32)

    copy(0).wait()
    plane(0, start)
    for z in range(1, depth + 1):
        if z >= 2:
            gram(z - 2)
        if z < depth:
            if (z - 1) % 3 == 0:
                for ahead in range(z, min(z + 3, depth)):
                    copy(ahead).wait()
            plane(z, emit)
        else:
            for y in range(rows_y):
                emit(z, y, None)
    gram(depth - 1)


def image_block(ft, smooth, m8, c8):
    rows, lanes = ft.shape
    shape = (rows // 8, 8, lanes)
    field = ft.astype(F32).reshape(shape)
    out = c8[None] * field - m8[None] * smooth.reshape(shape)
    return out.reshape(rows, lanes).astype(BF16)


def edge_kernel(
    rows_y, rows_x, scale,
    snapshots_ref, halo_ref, material_ref, occupied_ref, moduli_ref, weights_ref, gram_ref,
    out_ref,
    own, image, sem,
):
    depth, lanes, width = snapshots_ref.shape
    occupied = lambda t: occupied_ref[0, t]
    load = pltpu.make_async_copy(snapshots_ref.at[depth - 1], own, sem)
    load.start()
    shape = (8, lanes)
    place_y, place_x = lane_place(shape, rows_x)
    own_mask = brick_select(occupied, rows_y, rows_x, place_y, place_x)
    value = look_up(material_ref[depth - 8 :, :], moduli_ref[...].astype(F32))
    own_mod = jnp.broadcast_to(value[7:8], shape) * own_mask
    extra = halo_ref[lanes : lanes + 16, :].astype(F32)
    parts = [extra[part : part + 1, :] for part in range(lanes // width)]
    halo_mod = jnp.broadcast_to(jnp.concatenate(parts, axis=1), shape)
    halo_mask = jnp.where(halo_mod > 0.0, 1.0, 0.0)
    own_c = 0.25 * smooth_plane(halo_mod, rows_y, rows_x) * own_mask
    halo_c = 0.25 * smooth_plane(own_mod, rows_y, rows_x) * halo_mask
    halo_t = halo_ref[:lanes, :].T
    halo_on = halo_t * halo_mask[0:1].astype(BF16)
    load.wait()
    own_t = own[...].T
    own_on = own_t * own_mask[0:1].astype(BF16)
    for start, low, high in windows(lanes):
        block = slice(start, start + BLOCK)
        first = low - (start - EDGE)
        part = weights_ref[first : first + high - low, :]
        from_halo = jnp.dot(halo_on[:, low:high], part, preferred_element_type=F32)
        from_own = jnp.dot(own_on[:, low:high], part, preferred_element_type=F32)
        image[0, :, block] = image_block(
            own_t[:, block], from_halo, own_mod[:, block], own_c[:, block]
        )
        image[1, :, block] = image_block(
            halo_t[:, block], from_own, halo_mod[:, block], halo_c[:, block]
        )
    total = gram_ref[...]
    total += jnp.dot(image[0], own[...], preferred_element_type=F32)
    total += jnp.dot(image[1], halo_ref[:lanes, :], preferred_element_type=F32)
    out_ref[...] = (total + total.T) * scale


def scatter_sum(value, axis):
    count = lax.axis_size(axis)
    position = lax.axis_index(axis)
    own = value.shape[0] // count
    step = 1
    while step < count:
        value = value.reshape(-1, 2, own, value.shape[-1])
        side = (position // step) % 2
        keep = lax.dynamic_index_in_dim(value, side, 1, keepdims=False)
        give = lax.dynamic_index_in_dim(value, 1 - side, 1, keepdims=False)
        swap = [(device, device ^ step) for device in range(count)]
        value = keep + lax.ppermute(give, axis, swap)
        step *= 2
    return value.reshape(own, value.shape[-1])


def local(snapshots, material, occupancy, moduli):
    depth, rows_y, rows_x, width = snapshots.shape
    lanes = rows_y * rows_x
    owners = lax.axis_size("bricks")
    scale = 1.0 / (depth * lanes * owners)
    planes = snapshots.reshape(depth, lanes, width)
    moduli = moduli.reshape(1, -1)
    weights = plane_weights(rows_x)
    vmem = pl.BlockSpec(memory_space=pltpu.VMEM)
    smem = pl.BlockSpec(memory_space=pltpu.SMEM)
    hbm = pl.BlockSpec(memory_space=pltpu.HBM)
    reach = BLOCK + 2 * rows_x

    packed = pl.pallas_call(
        lambda *refs: pack_kernel(rows_y, rows_x, *refs),
        in_specs=[hbm, vmem, smem, vmem],
        out_specs=hbm,
        out_shape=jax.ShapeDtypeStruct((lanes + 16, width), BF16),
        scratch_shapes=[
            pltpu.VMEM((16, width), F32),
            pltpu.VMEM((16, width), BF16),
            pltpu.SemaphoreType.DMA((2,)),
        ],
        compiler_params=pltpu.CompilerParams(vmem_limit_bytes=56 << 20),
        name="pack",
    )(planes, material, occupancy, moduli)

    halo = lax.ppermute(packed, "bricks", [(i + 1, i) for i in range(owners - 1)])

    gram = pl.pallas_call(
        lambda *refs: main_kernel(rows_y, rows_x, *refs),
        in_specs=[hbm, vmem, smem, vmem, vmem],
        out_specs=vmem,
        out_shape=jax.ShapeDtypeStruct((width, width), F32),
        scratch_shapes=[
            pltpu.VMEM((depth, lanes, width), BF16),
            pltpu.VMEM((2, reach, BLOCK), BF16),
            pltpu.VMEM((lanes, width), F32),
            pltpu.VMEM((lanes, width), F32),
            pltpu.VMEM((2, lanes, width), BF16),
            pltpu.VMEM((depth, 16, lanes), BF16),
            pltpu.VMEM((lanes, 128), F32),
            pltpu.VMEM((lanes // BLOCK, reach, BLOCK), BF16),
            pltpu.SemaphoreType.DMA((depth,)),
        ],
        compiler_params=pltpu.CompilerParams(vmem_limit_bytes=56 << 20),
        cost_estimate=pl.CostEstimate(
            flops=6 * depth * lanes * width * width,
            bytes_accessed=2 * depth * lanes * width,
            transcendentals=0,
        ),
        name="interior",
    )(planes, material, occupancy, moduli, weights)

    share = pl.pallas_call(
        lambda *refs: edge_kernel(rows_y, rows_x, scale, *refs),
        in_specs=[hbm, vmem, vmem, smem, vmem, vmem, vmem],
        out_specs=vmem,
        out_shape=jax.ShapeDtypeStruct((width, width), F32),
        scratch_shapes=[
            pltpu.VMEM((lanes, width), BF16),
            pltpu.VMEM((2, width, lanes), BF16),
            pltpu.SemaphoreType.DMA(()),
        ],
        compiler_params=pltpu.CompilerParams(vmem_limit_bytes=24 << 20),
        cost_estimate=pl.CostEstimate(
            flops=12 * lanes * width * width, bytes_accessed=4 * lanes * width, transcendentals=0
        ),
        name="edge",
    )(planes, halo, material, occupancy, moduli, weights, gram)
    return scatter_sum(share, "bricks")


def solution(mesh):
    in_specs = (
        P(("groups", "bricks"), None, None, None),
        P(("groups", "bricks"), None),
        P(("groups", "bricks"), None),
        P(),
    )
    out_specs = P(("groups", "bricks"), None)
    return jax.shard_map(local, mesh=mesh, in_specs=in_specs, out_specs=out_specs, check_vma=False)
```

time: 40.2 us -> 55.6 us (1.38)
  Pallas kernels: 17.5 us -> 31.9 us
  local copies, waits for them, and re-layouts: 3.44 us -> 4.4 us
    pallas_call x1, Pallas kernels: 2.2 us -> 17.9 us  [local(): pl.pallas_call(lambda *refs: pack_kernel(rows_y, rows_x, *refs), in_specs...]
    pallas_call x1, Pallas kernels: 13.1 us -> 11.9 us  [local(): pl.pallas_call(lambda *refs: main_kernel(rows_y, rows_x, *refs), in_specs...]
    unnamed x12, local copies, waits for them, and re-layouts: 3.4 us -> 4.35 us
  transfers between devices with their start and end apart: 5 -> 5, of which waited for: 4 -> 4; matrix products, arithmetic and copies ran while one was open for 0% -> 0% of each run, Pallas kernels for 33% -> 21%
where the time goes in v2:
time: 55.6 us; the launch traced here: 55.4 us
  Pallas kernels  31.9 us (57%)
  starting transfers between devices  11.1 us (20%)
  waiting for transfers between devices  7.21 us (13%)
  local copies, waits for them, and re-layouts  4.4 us (8%)
  other arithmetic  0.64 us (1%)
    pallas_call x1, Pallas kernels, local(): pl.pallas_call(lambda *refs: pack_kernel(rows_y, rows_x, *refs), in_specs...  17.9 us
    pallas_call x1, Pallas kernels, local(): pl.pallas_call(lambda *refs: main_kernel(rows_y, rows_x, *refs), in_specs...  11.9 us
    ppermute x4, starting transfers between devices, scatter_sum(): value = keep + lax.ppermute(give, axis, swap)  9.8 us
    ppermute x4, waiting for transfers between devices, scatter_sum(): value = keep + lax.ppermute(give, axis, swap)  7.2 us
    unnamed x12, local copies, waits for them, and re-layouts  4.35 us
    pallas_call x1, Pallas kernels, local(): pl.pallas_call(lambda *refs: edge_kernel(rows_y, rows_x, scale, *refs), i...  2.15 us
    ppermute x1, starting transfers between devices, local(): lax.ppermute(packed, 'bricks', [(i + 1, i) for i in range(owners - 1)])  1.29 us
  transfers between devices with their start and end apart: 5, of which 4 were waited for; matrix products, arithmetic and copies ran while one was open for 0% of the time, Pallas kernels for 21%

profile of v2, /device:TPU:0, one launch (start us, length us, event | category | flops | bytes accessed | tf_op | source)
XLA Modules:
  0.0 55.4 jit_solution(17168238937263290364)
XLA Ops:
  0.0 17.9 %pack.1 = bf16[1040,256]{1,0:T(8,128)(2,1)} custom-call(bf16[16,1024,256]{2,1,0:T(8,128)(2,1)} %bitcast.19, s32[16,1024]{1,0:T(8,128)} %refs_2_.5, s32[1,4]{1,0:T(1,128)} %refs_3_.1, bf16[1,16]{1,0:T(2,128)(2,1)} %bitcast.24), custom_call_target="tpu_custom_call" | custom-call | tf_op jit(solution)/shard_map/pack/pallas_call | solution.py:270
  17.9 1.3 %collective-permute-start = (bf16[1040,256]{1,0:T(8,128)(2,1)}, bf16[1040,256]{1,0:T(8,128)(2,1)S(1)}, u32[]{:S(2)}, u32[]{:S(2)}) collective-permute-start(bf16[1040,256]{1,0:T(8,128)(2,1)} %pack.1), channel_id=1, source_target_pairs={{1,0},{2,1},{3,2},{4,3},{5,4},{6,5},{7,6},{8,7},{9,8},{10,9},{11,1... | collective-permute-start | bytes 1597448 | tf_op jit(solution)/shard_map/ppermute | solution.py:284
  19.2 0.0 copy-start.1
  19.2 0.0 copy-start.2
  19.2 0.0 copy-start.4
  19.2 0.0 copy-start.5
  19.2 11.9 %interior.1.refs_6_ = f32[256,256]{1,0:T(8,128)} custom-call(bf16[16,1024,256]{2,1,0:T(8,128)(2,1)} %bitcast.20, s32[16,1024]{1,0:T(8,128)} %refs_2_.5, s32[1,4]{1,0:T(1,128)} %refs_3_.1, bf16[1,16]{1,0:T(2,128)(2,1)} %bitcast.25, bf16[512,256]{1,0:T(8,128)(2,1)} %constant.99.clone.refs_4_.refs_5_), custom_call_target="tpu_custom_call" | custom-call | flops 6442450944 | bytes 8388608 | tf_op jit(solution)/shard_map/interior/pallas_call | solution.py:286
  31.1 0.0 collective-permute-done.refs_1_
  31.1 0.0 copy-done.1
  31.1 0.0 copy-done.2
  31.1 0.0 copy-done.4
  31.1 0.0 copy-done.5
  31.1 0.0 copy-start
  31.2 3.4 %copy-done = bf16[16,32,32,256]{3,2,1,0:T(8,128)(2,1)S(1)} copy-done((bf16[16,32,32,256]{3,2,1,0:T(8,128)(2,1)S(1)}, bf16[16,32,32,256]{3,2,1,0:T(8,128)(2,1)}, u32[]{:S(2)}) %copy-start) | copy-done | bytes 8388632
  34.5 0.0 copy-start.3
  34.5 0.9 %copy-done.3 = f32[256,256]{1,0:T(8,128)S(1)} copy-done((f32[256,256]{1,0:T(8,128)S(1)}, f32[256,256]{1,0:T(8,128)}, u32[]{:S(2)}) %copy-start.3) | copy-done | bytes 262168
  35.5 2.1 %edge.1 = f32[256,256]{1,0:T(8,128)S(1)} custom-call(bf16[16,1024,256]{2,1,0:T(8,128)(2,1)S(1)} %bitcast.21, bf16[1040,256]{1,0:T(8,128)(2,1)S(1)} %collective-permute-done.refs_1_, s32[16,1024]{1,0:T(8,128)S(1)} %copy-done.1, s32[1,4]{1,0:T(1,128)S(1)} %copy-done.4, bf16[1,16]{1,0:T(2,128)(2,1)S(1)} %bitcast.26, bf16[512,256]{1,0:T(8,128)(2,1)S(1)} %copy-done.2, ...), custom_call_target="tpu_custom_call" | custom-call | flops 805306368 | bytes 1048576 | tf_op jit(solution)/shard_map/edge/pallas_call | solution.py:311
  37.7 1.2 %collective-permute-start.1 = (f32[8,16,256]{2,1,0:T(8,128)S(1)}, f32[8,16,256]{2,1,0:T(8,128)S(1)}, u32[]{:S(2)}, u32[]{:S(2)}) collective-permute-start(f32[8,16,256]{2,1,0:T(8,128)S(1)} %dynamic-slice_bitcast_fusion), channel_id=1, source_target_pairs={{0,1},{1,0},{2,3},{3,2},{4,5},{5,4},{6,7},{7,6},{8,9},{9,8},{10,11... | collective-permute-start | bytes 393224 | tf_op jit(solution)/shard_map/ppermute | solution.py:252
  38.9 1.0 %collective-permute-done.1 = f32[8,16,256]{2,1,0:T(8,128)S(1)} collective-permute-done((f32[8,16,256]{2,1,0:T(8,128)S(1)}, f32[8,16,256]{2,1,0:T(8,128)S(1)}, u32[]{:S(2)}, u32[]{:S(2)}) %collective-permute-start.1) | collective-permute-done | bytes 131104 | tf_op jit(solution)/shard_map/ppermute | solution.py:252
  39.9 3.0 %collective-permute-start.2 = (f32[4,16,256]{2,1,0:T(8,128)S(1)}, f32[4,16,256]{2,1,0:T(8,128)S(1)}, u32[]{:S(2)}, u32[]{:S(2)}) collective-permute-start(f32[4,16,256]{2,1,0:T(8,128)S(1)} %dynamic-slice_bitcast_fusion.1), channel_id=1, source_target_pairs={{0,2},{1,3},{2,0},{3,1},{4,6},{5,7},{6,4},{7,5},{8,10},{9,11},{10,... | collective-permute-start | bytes 196616 | tf_op jit(solution)/shard_map/ppermute | solution.py:252
  42.9 2.6 %collective-permute-done.2 = f32[4,16,256]{2,1,0:T(8,128)S(1)} collective-permute-done((f32[4,16,256]{2,1,0:T(8,128)S(1)}, f32[4,16,256]{2,1,0:T(8,128)S(1)}, u32[]{:S(2)}, u32[]{:S(2)}) %collective-permute-start.2) | collective-permute-done | bytes 65568 | tf_op jit(solution)/shard_map/ppermute | solution.py:252
  45.6 2.5 %collective-permute-start.3 = (f32[2,16,256]{2,1,0:T(8,128)S(1)}, f32[2,16,256]{2,1,0:T(8,128)S(1)}, u32[]{:S(2)}, u32[]{:S(2)}) collective-permute-start(f32[2,16,256]{2,1,0:T(8,128)S(1)} %dynamic-slice_bitcast_fusion.2), channel_id=1, source_target_pairs={{0,4},{1,5},{2,6},{3,7},{4,0},{5,1},{6,2},{7,3},{8,12},{9,13},{10,... | collective-permute-start | bytes 98312 | tf_op jit(solution)/shard_map/ppermute | solution.py:252
  48.0 1.9 %collective-permute-done.3 = f32[2,16,256]{2,1,0:T(8,128)S(1)} collective-permute-done((f32[2,16,256]{2,1,0:T(8,128)S(1)}, f32[2,16,256]{2,1,0:T(8,128)S(1)}, u32[]{:S(2)}, u32[]{:S(2)}) %collective-permute-start.3) | collective-permute-done | bytes 32800 | tf_op jit(solution)/shard_map/ppermute | solution.py:252
  49.9 3.1 %collective-permute-start.4 = (f32[1,16,256]{2,1,0:T(8,128)S(1)}, f32[1,16,256]{2,1,0:T(8,128)S(1)}, u32[]{:S(2)}, u32[]{:S(2)}) collective-permute-start(f32[1,16,256]{2,1,0:T(8,128)S(1)} %constant_dynamic-slice_fusion), channel_id=1, source_target_pairs={{0,8},{1,9},{2,10},{3,11},{4,12},{5,13},{6,14},{7,15},{8,0},{9,1},... | collective-permute-start | bytes 49160 | tf_op jit(solution)/shard_map/ppermute | solution.py:252
  53.0 1.7 %collective-permute-done.4 = f32[1,16,256]{2,1,0:T(8,128)S(1)} collective-permute-done((f32[1,16,256]{2,1,0:T(8,128)S(1)}, f32[1,16,256]{2,1,0:T(8,128)S(1)}, u32[]{:S(2)}, u32[]{:S(2)}) %collective-permute-start.4) | collective-permute-done | bytes 16416 | tf_op jit(solution)/shard_map/ppermute | solution.py:252
  54.8 0.6 %add_bitcast_fusion = f32[16,256]{1,0:T(8,128)} fusion(f32[1,16,256]{2,1,0:T(8,128)S(1)} %collective-permute-done.4, f32[2,16,256]{2,1,0:T(8,128)S(1)} %bitcast_add_fusion.2, s32[]{:T(128)S(6)} %select_n.71), kind=kLoop, calls=%fused_computation.6 | loop fusion | flops 4096 | bytes 49156 | tf_op jit(solution)/shard_map/reshape | solution.py:254
  (7 shorter events, 0.1 us)
Async XLA Ops:
  17.9 13.2 %collective-permute-start = (bf16[1040,256]{1,0:T(8,128)(2,1)}, bf16[1040,256]{1,0:T(8,128)(2,1)S(1)}, u32[]{:S(2)}, u32[]{:S(2)}) collective-permute-start(bf16[1040,256]{1,0:T(8,128)(2,1)} %pack.1), channel_id=1, source_target_pairs={{1,0},{2,1},{3,2},{4,3},{5,4},{6,5},{7,6},{8,7},{9,8},{10,9},{11,1... | collective-permute-start | bytes 1597448 | tf_op jit(solution)/shard_map/ppermute | solution.py:284
  19.2 11.9 %copy-start.1 = (s32[16,1024]{1,0:T(8,128)S(1)}, s32[16,1024]{1,0:T(8,128)}, u32[]{:S(2)}) copy-start(s32[16,1024]{1,0:T(8,128)} %refs_2_.5) | copy-start | bytes 196612
  19.2 11.9 %copy-start.2 = (bf16[512,256]{1,0:T(8,128)(2,1)S(1)}, bf16[512,256]{1,0:T(8,128)(2,1)}, u32[]{:S(2)}) copy-start(bf16[512,256]{1,0:T(8,128)(2,1)} %constant.99.clone.refs_4_.refs_5_) | copy-start | bytes 786436
  19.2 11.9 %copy-start.4 = (s32[1,4]{1,0:T(1,128)S(1)}, s32[1,4]{1,0:T(1,128)}, u32[]{:S(2)}) copy-start(s32[1,4]{1,0:T(1,128)} %refs_3_.1) | copy-start | bytes 52
  19.2 11.9 %copy-start.5 = (bf16[16]{0:T(256)(128)(2,1)S(1)}, bf16[16]{0:T(256)(128)(2,1)}, u32[]{:S(2)}) copy-start(bf16[16]{0:T(256)(128)(2,1)} %param.8) | copy-start | bytes 100
  31.1 3.4 %copy-start = (bf16[16,32,32,256]{3,2,1,0:T(8,128)(2,1)S(1)}, bf16[16,32,32,256]{3,2,1,0:T(8,128)(2,1)}, u32[]{:S(2)}) copy-start(bf16[16,32,32,256]{3,2,1,0:T(8,128)(2,1)} %param.5) | copy-start | bytes 25165828
  34.5 0.9 %copy-start.3 = (f32[256,256]{1,0:T(8,128)S(1)}, f32[256,256]{1,0:T(8,128)}, u32[]{:S(2)}) copy-start(f32[256,256]{1,0:T(8,128)} %interior.1.refs_6_) | copy-start | bytes 786436
  37.7 2.2 %collective-permute-start.1 = (f32[8,16,256]{2,1,0:T(8,128)S(1)}, f32[8,16,256]{2,1,0:T(8,128)S(1)}, u32[]{:S(2)}, u32[]{:S(2)}) collective-permute-start(f32[8,16,256]{2,1,0:T(8,128)S(1)} %dynamic-slice_bitcast_fusion), channel_id=1, source_target_pairs={{0,1},{1,0},{2,3},{3,2},{4,5},{5,4},{6,7},{7,6},{8,9},{9,8},{10,11... | collective-permute-start | bytes 393224 | tf_op jit(solution)/shard_map/ppermute | solution.py:252
  39.9 5.7 %collective-permute-start.2 = (f32[4,16,256]{2,1,0:T(8,128)S(1)}, f32[4,16,256]{2,1,0:T(8,128)S(1)}, u32[]{:S(2)}, u32[]{:S(2)}) collective-permute-start(f32[4,16,256]{2,1,0:T(8,128)S(1)} %dynamic-slice_bitcast_fusion.1), channel_id=1, source_target_pairs={{0,2},{1,3},{2,0},{3,1},{4,6},{5,7},{6,4},{7,5},{8,10},{9,11},{10,... | collective-permute-start | bytes 196616 | tf_op jit(solution)/shard_map/ppermute | solution.py:252
  45.6 4.4 %collective-permute-start.3 = (f32[2,16,256]{2,1,0:T(8,128)S(1)}, f32[2,16,256]{2,1,0:T(8,128)S(1)}, u32[]{:S(2)}, u32[]{:S(2)}) collective-permute-start(f32[2,16,256]{2,1,0:T(8,128)S(1)} %dynamic-slice_bitcast_fusion.2), channel_id=1, source_target_pairs={{0,4},{1,5},{2,6},{3,7},{4,0},{5,1},{6,2},{7,3},{8,12},{9,13},{10,... | collective-permute-start | bytes 98312 | tf_op jit(solution)/shard_map/ppermute | solution.py:252
  49.9 4.8 %collective-permute-start.4 = (f32[1,16,256]{2,1,0:T(8,128)S(1)}, f32[1,16,256]{2,1,0:T(8,128)S(1)}, u32[]{:S(2)}, u32[]{:S(2)}) collective-permute-start(f32[1,16,256]{2,1,0:T(8,128)S(1)} %constant_dynamic-slice_fusion), channel_id=1, source_target_pairs={{0,8},{1,9},{2,10},{3,11},{4,12},{5,13},{6,14},{7,15},{8,0},{9,1},... | collective-permute-start | bytes 49160 | tf_op jit(solution)/shard_map/ppermute | solution.py:252

commit v3 on v2

--- a/solution.py
+++ b/solution.py
@@ -62,10 +62,10 @@
 
 
 def pack_kernel(
-    rows_y, rows_x, snapshots_ref, material_ref, occupied_ref, moduli_ref, out_ref, rows, packed, sems
+    rows_y, rows_x, snapshots_ref, material_ref, occupied_ref, moduli_ref, out_ref, rows, sem
 ):
     lanes, width = snapshots_ref.shape[1:]
-    plane = pltpu.make_async_copy(snapshots_ref.at[0], out_ref.at[pl.ds(0, lanes)], sems.at[0])
+    plane = pltpu.make_async_copy(snapshots_ref.at[0], out_ref.at[pl.ds(0, lanes)], sem)
     plane.start()
     occupied = lambda t: occupied_ref[0, t]
     place_y, place_x = lane_place((8, lanes), rows_x)
@@ -74,18 +74,15 @@
     rows[...] = jnp.zeros_like(rows)
     for part in range(lanes // width):
         rows[part : part + 1, :] = value[0:1, part * width : (part + 1) * width]
-    packed[...] = rows[...].astype(BF16)
-    extra = pltpu.make_async_copy(packed, out_ref.at[pl.ds(lanes, 16)], sems.at[1])
-    extra.start()
+    out_ref[lanes : lanes + 16, :] = rows[...].astype(BF16)
     plane.wait()
-    extra.wait()
 
 
 def main_kernel(
     rows_y, rows_x,
     snapshots_ref, material_ref, occupied_ref, moduli_ref, weights_ref,
-    out_ref,
-    field, lhs, last, pair, image, modulus_rows, center_columns, masked, sems,
+    out_ref, top_ref,
+    field, lhs, last, pair, image, modulus_rows, center_columns, masked, sems, top_sem,
 ):
     depth, lanes, width = snapshots_ref.shape
     blocks = lanes // BLOCK
@@ -170,6 +167,7 @@
     def gram(z):
         out_ref[...] += jnp.dot(image[z % 2].T, field[z], preferred_element_type=F32)
 
+    top = pltpu.make_async_copy(field.at[depth - 1], top_ref, top_sem)
     copy(0).wait()
     plane(0, start)
     for z in range(1, depth + 1):
@@ -179,11 +177,14 @@
             if (z - 1) % 3 == 0:
                 for ahead in range(z, min(z + 3, depth)):
                     copy(ahead).wait()
+                    if ahead == depth - 1:
+                        top.start()
             plane(z, emit)
         else:
             for y in range(rows_y):
                 emit(z, y, None)
     gram(depth - 1)
+    top.wait()
 
 
 def image_block(ft, smooth, m8, c8):
@@ -196,14 +197,13 @@
 
 def edge_kernel(
     rows_y, rows_x, scale,
-    snapshots_ref, halo_ref, material_ref, occupied_ref, moduli_ref, weights_ref, gram_ref,
+    own, halo_ref, material_ref, occupied_ref, moduli_ref, weights_ref, gram_ref,
     out_ref,
-    own, image, sem,
+    image,
 ):
-    depth, lanes, width = snapshots_ref.shape
+    lanes, width = own.shape
+    depth = material_ref.shape[0]
     occupied = lambda t: occupied_ref[0, t]
-    load = pltpu.make_async_copy(snapshots_ref.at[depth - 1], own, sem)
-    load.start()
     shape = (8, lanes)
     place_y, place_x = lane_place(shape, rows_x)
     own_mask = brick_select(occupied, rows_y, rows_x, place_y, place_x)
@@ -217,7 +217,6 @@
     halo_c = 0.25 * smooth_plane(own_mod, rows_y, rows_x) * halo_mask
     halo_t = halo_ref[:lanes, :].T
     halo_on = halo_t * halo_mask[0:1].astype(BF16)
-    load.wait()
     own_t = own[...].T
     own_on = own_t * own_mask[0:1].astype(BF16)
     for start, low, high in windows(lanes):
@@ -270,24 +269,23 @@
     packed = pl.pallas_call(
         lambda *refs: pack_kernel(rows_y, rows_x, *refs),
         in_specs=[hbm, vmem, smem, vmem],
-        out_specs=hbm,
+        out_specs=vmem,
         out_shape=jax.ShapeDtypeStruct((lanes + 16, width), BF16),
-        scratch_shapes=[
-            pltpu.VMEM((16, width), F32),
-            pltpu.VMEM((16, width), BF16),
-            pltpu.SemaphoreType.DMA((2,)),
-        ],
-        compiler_params=pltpu.CompilerParams(vmem_limit_bytes=56 << 20),
+        scratch_shapes=[pltpu.VMEM((16, width), F32), pltpu.SemaphoreType.DMA(())],
+        compiler_params=pltpu.CompilerParams(vmem_limit_bytes=52 << 20),
         name="pack",
     )(planes, material, occupancy, moduli)
 
     halo = lax.ppermute(packed, "bricks", [(i + 1, i) for i in range(owners - 1)])
 
-    gram = pl.pallas_call(
+    gram, top = pl.pallas_call(
         lambda *refs: main_kernel(rows_y, rows_x, *refs),
         in_specs=[hbm, vmem, smem, vmem, vmem],
-        out_specs=vmem,
-        out_shape=jax.ShapeDtypeStruct((width, width), F32),
+        out_specs=(vmem, hbm),
+        out_shape=(
+            jax.ShapeDtypeStruct((width, width), F32),
+            jax.ShapeDtypeStruct((lanes, width), BF16),
+        ),
         scratch_shapes=[
             pltpu.VMEM((depth, lanes, width), BF16),
             pltpu.VMEM((2, reach, BLOCK), BF16),
@@ -298,8 +296,9 @@
             pltpu.VMEM((lanes, 128), F32),
             pltpu.VMEM((lanes // BLOCK, reach, BLOCK), BF16),
             pltpu.SemaphoreType.DMA((depth,)),
+            pltpu.SemaphoreType.DMA(()),
         ],
-        compiler_params=pltpu.CompilerParams(vmem_limit_bytes=56 << 20),
+        compiler_params=pltpu.CompilerParams(vmem_limit_bytes=52 << 20),
         cost_estimate=pl.CostEstimate(
             flops=6 * depth * lanes * width * width,
             bytes_accessed=2 * depth * lanes * width,
@@ -310,20 +309,16 @@
 
     share = pl.pallas_call(
         lambda *refs: edge_kernel(rows_y, rows_x, scale, *refs),
-        in_specs=[hbm, vmem, vmem, smem, vmem, vmem, vmem],
+        in_specs=[vmem, vmem, vmem, smem, vmem, vmem, vmem],
         out_specs=vmem,
         out_shape=jax.ShapeDtypeStruct((width, width), F32),
-        scratch_shapes=[
-            pltpu.VMEM((lanes, width), BF16),
-            pltpu.VMEM((2, width, lanes), BF16),
-            pltpu.SemaphoreType.DMA(()),
-        ],
-        compiler_params=pltpu.CompilerParams(vmem_limit_bytes=24 << 20),
+        scratch_shapes=[pltpu.VMEM((2, width, lanes), BF16)],
+        compiler_params=pltpu.CompilerParams(vmem_limit_bytes=40 << 20),
         cost_estimate=pl.CostEstimate(
             flops=12 * lanes * width * width, bytes_accessed=4 * lanes * width, transcendentals=0
         ),
         name="edge",
-    )(planes, halo, material, occupancy, moduli, weights, gram)
+    )(top, halo, material, occupancy, moduli, weights, gram)
     return scatter_sum(share, "bricks")
 
 

time: 55.6 us -> 35.7 us (0.64)
  Pallas kernels: 31.9 us -> 14.1 us
  local copies, waits for them, and re-layouts: 4.4 us -> 2.24 us
    pallas_call x1, Pallas kernels: 17.9 us -> 1.59 us  [local(): pl.pallas_call(lambda *refs: pack_kernel(rows_y, rows_x, *refs), in_specs...]
    unnamed x12 -> x14, local copies, waits for them, and re-layouts: 4.35 us -> 2.19 us
    pallas_call x1, Pallas kernels: 11.9 us -> 10.6 us  [local(): pl.pallas_call(lambda *refs: main_kernel(rows_y, rows_x, *refs), in_specs...]
  transfers between devices with their start and end apart: 5 -> 5, of which waited for: 4 -> 4; matrix products, arithmetic and copies ran while one was open for 0% -> 0% of each run, Pallas kernels for 21% -> 30%
where the time goes in v3:
time: 35.7 us; the launch traced here: 35.5 us
  Pallas kernels  14.1 us (39%)
  starting transfers between devices  11.1 us (31%)
  waiting for transfers between devices  7.21 us (20%)
  local copies, waits for them, and re-layouts  2.24 us (6%)
  other arithmetic  0.64 us (2%)
    pallas_call x1, Pallas kernels, local(): pl.pallas_call(lambda *refs: main_kernel(rows_y, rows_x, *refs), in_specs...  10.6 us
    ppermute x4, starting transfers between devices, scatter_sum(): value = keep + lax.ppermute(give, axis, swap)  9.8 us
    ppermute x4, waiting for transfers between devices, scatter_sum(): value = keep + lax.ppermute(give, axis, swap)  7.2 us
    unnamed x14, local copies, waits for them, and re-layouts  2.19 us
    pallas_call x1, Pallas kernels, local(): pl.pallas_call(lambda *refs: edge_kernel(rows_y, rows_x, scale, *refs), i...  1.98 us
    pallas_call x1, Pallas kernels, local(): pl.pallas_call(lambda *refs: pack_kernel(rows_y, rows_x, *refs), in_specs...  1.59 us
    ppermute x1, starting transfers between devices, local(): lax.ppermute(packed, 'bricks', [(i + 1, i) for i in range(owners - 1)])  1.29 us
  transfers between devices with their start and end apart: 5, of which 4 were waited for; matrix products, arithmetic and copies ran while one was open for 0% of the time, Pallas kernels for 30%

profile of v3, /device:TPU:0, one launch (start us, length us, event | category | flops | bytes accessed | tf_op | source)
XLA Modules:
  0.0 35.5 jit_solution(12428299167402595969)
XLA Ops:
  0.0 0.0 copy-start.3
  0.0 0.0 copy-start.5
  0.0 0.0 copy-start
  0.0 0.9 %copy-done = s32[16,1024]{1,0:T(8,128)S(1)} copy-done((s32[16,1024]{1,0:T(8,128)S(1)}, s32[16,1024]{1,0:T(8,128)}, u32[]{:S(2)}) %copy-start) | copy-done | bytes 65560
  0.9 0.0 copy-start.2
  0.9 0.7 %copy-done.2 = s32[1,4]{1,0:T(1,128)S(1)} copy-done((s32[1,4]{1,0:T(1,128)S(1)}, s32[1,4]{1,0:T(1,128)}, u32[]{:S(2)}) %copy-start.2) | copy-done | bytes 40
  1.5 0.0 copy-start.4
  1.5 0.7 %copy-done.4 = bf16[16]{0:T(256)(128)(2,1)S(1)} copy-done((bf16[16]{0:T(256)(128)(2,1)S(1)}, bf16[16]{0:T(256)(128)(2,1)}, u32[]{:S(2)}) %copy-start.4) | copy-done | bytes 56
  2.2 0.0 copy-start.1
  2.2 0.0 copy-start.6
  2.2 1.6 %pack.1 = bf16[1040,256]{1,0:T(8,128)(2,1)S(1)} custom-call(bf16[16,1024,256]{2,1,0:T(8,128)(2,1)} %bitcast.24, s32[16,1024]{1,0:T(8,128)S(1)} %copy-done, s32[1,4]{1,0:T(1,128)S(1)} %copy-done.2, bf16[1,16]{1,0:T(2,128)(2,1)S(1)} %bitcast.21), custom_call_target="tpu_custom_call" | custom-call | tf_op jit(solution)/shard_map/pack/pallas_call | solution.py:269
  3.8 1.3 %collective-permute-start = (bf16[1040,256]{1,0:T(8,128)(2,1)S(1)}, bf16[1040,256]{1,0:T(8,128)(2,1)S(1)}, u32[]{:S(2)}, u32[]{:S(2)}) collective-permute-start(bf16[1040,256]{1,0:T(8,128)(2,1)S(1)} %pack.1), channel_id=1, source_target_pairs={{1,0},{2,1},{3,2},{4,3},{5,4},{6,5},{7,6},{8,7},{9,8},{10,9},{11,1... | collective-permute-start | bytes 1597448 | tf_op jit(solution)/shard_map/ppermute | solution.py:279
  5.1 0.0 copy-done.3
  5.1 0.0 copy-done.5
  5.1 0.0 copy-done.1
  5.1 0.0 copy-done.6
  5.1 10.6 %interior.1 = (f32[256,256]{1,0:T(8,128)S(1)}, bf16[1024,256]{1,0:T(8,128)(2,1)S(1)}) custom-call(bf16[16,1024,256]{2,1,0:T(8,128)(2,1)} %bitcast.25, s32[16,1024]{1,0:T(8,128)S(1)} %copy-done.1, s32[1,4]{1,0:T(1,128)S(1)} %copy-done.3, bf16[1,16]{1,0:T(2,128)(2,1)S(1)} %bitcast.22, bf16[512,256]{1,0:T(8,128)(2,1)S(1)} %copy-done.6), custom_call_target="tpu_custom_call" | custom-call | flops 6442450944 | bytes 8388608 | tf_op jit(solution)/shard_map/interior/pallas_call | solution.py:281
  15.7 0.0 collective-permute-done.refs_1_
  15.7 2.0 %edge.1 = f32[256,256]{1,0:T(8,128)S(1)} custom-call(bf16[1024,256]{1,0:T(8,128)(2,1)S(1)} %get-tuple-element.7.refs_0_, bf16[1040,256]{1,0:T(8,128)(2,1)S(1)} %collective-permute-done.refs_1_, s32[16,1024]{1,0:T(8,128)S(1)} %copy-done.1, s32[1,4]{1,0:T(1,128)S(1)} %copy-done.3, bf16[1,16]{1,0:T(2,128)(2,1)S(1)} %bitcast.23, bf16[512,256]{1,0:T(8,128)(2,1)S(1)} %copy-done.6, ...), custom_call_target="tpu_custom_call" | custom-call | flops 805306368 | bytes 1048576 | tf_op jit(solution)/shard_map/edge/pallas_call | solution.py:310
  17.8 1.2 %collective-permute-start.1 = (f32[8,16,256]{2,1,0:T(8,128)S(1)}, f32[8,16,256]{2,1,0:T(8,128)S(1)}, u32[]{:S(2)}, u32[]{:S(2)}) collective-permute-start(f32[8,16,256]{2,1,0:T(8,128)S(1)} %dynamic-slice_bitcast_fusion), channel_id=1, source_target_pairs={{0,1},{1,0},{2,3},{3,2},{4,5},{5,4},{6,7},{7,6},{8,9},{9,8},{10,11... | collective-permute-start | bytes 393224 | tf_op jit(solution)/shard_map/ppermute | solution.py:251
  19.0 1.0 %collective-permute-done.1 = f32[8,16,256]{2,1,0:T(8,128)S(1)} collective-permute-done((f32[8,16,256]{2,1,0:T(8,128)S(1)}, f32[8,16,256]{2,1,0:T(8,128)S(1)}, u32[]{:S(2)}, u32[]{:S(2)}) %collective-permute-start.1) | collective-permute-done | bytes 131104 | tf_op jit(solution)/shard_map/ppermute | solution.py:251
  20.0 3.0 %collective-permute-start.2 = (f32[4,16,256]{2,1,0:T(8,128)S(1)}, f32[4,16,256]{2,1,0:T(8,128)S(1)}, u32[]{:S(2)}, u32[]{:S(2)}) collective-permute-start(f32[4,16,256]{2,1,0:T(8,128)S(1)} %dynamic-slice_bitcast_fusion.1), channel_id=1, source_target_pairs={{0,2},{1,3},{2,0},{3,1},{4,6},{5,7},{6,4},{7,5},{8,10},{9,11},{10,... | collective-permute-start | bytes 196616 | tf_op jit(solution)/shard_map/ppermute | solution.py:251
  23.0 2.6 %collective-permute-done.2 = f32[4,16,256]{2,1,0:T(8,128)S(1)} collective-permute-done((f32[4,16,256]{2,1,0:T(8,128)S(1)}, f32[4,16,256]{2,1,0:T(8,128)S(1)}, u32[]{:S(2)}, u32[]{:S(2)}) %collective-permute-start.2) | collective-permute-done | bytes 65568 | tf_op jit(solution)/shard_map/ppermute | solution.py:251
  25.7 2.5 %collective-permute-start.3 = (f32[2,16,256]{2,1,0:T(8,128)S(1)}, f32[2,16,256]{2,1,0:T(8,128)S(1)}, u32[]{:S(2)}, u32[]{:S(2)}) collective-permute-start(f32[2,16,256]{2,1,0:T(8,128)S(1)} %dynamic-slice_bitcast_fusion.2), channel_id=1, source_target_pairs={{0,4},{1,5},{2,6},{3,7},{4,0},{5,1},{6,2},{7,3},{8,12},{9,13},{10,... | collective-permute-start | bytes 98312 | tf_op jit(solution)/shard_map/ppermute | solution.py:251
  28.1 1.9 %collective-permute-done.3 = f32[2,16,256]{2,1,0:T(8,128)S(1)} collective-permute-done((f32[2,16,256]{2,1,0:T(8,128)S(1)}, f32[2,16,256]{2,1,0:T(8,128)S(1)}, u32[]{:S(2)}, u32[]{:S(2)}) %collective-permute-start.3) | collective-permute-done | bytes 32800 | tf_op jit(solution)/shard_map/ppermute | solution.py:251
  30.0 3.1 %collective-permute-start.4 = (f32[1,16,256]{2,1,0:T(8,128)S(1)}, f32[1,16,256]{2,1,0:T(8,128)S(1)}, u32[]{:S(2)}, u32[]{:S(2)}) collective-permute-start(f32[1,16,256]{2,1,0:T(8,128)S(1)} %constant_dynamic-slice_fusion), channel_id=1, source_target_pairs={{0,8},{1,9},{2,10},{3,11},{4,12},{5,13},{6,14},{7,15},{8,0},{9,1},... | collective-permute-start | bytes 49160 | tf_op jit(solution)/shard_map/ppermute | solution.py:251
  33.1 1.7 %collective-permute-done.4 = f32[1,16,256]{2,1,0:T(8,128)S(1)} collective-permute-done((f32[1,16,256]{2,1,0:T(8,128)S(1)}, f32[1,16,256]{2,1,0:T(8,128)S(1)}, u32[]{:S(2)}, u32[]{:S(2)}) %collective-permute-start.4) | collective-permute-done | bytes 16416 | tf_op jit(solution)/shard_map/ppermute | solution.py:251
  34.8 0.6 %add_bitcast_fusion = f32[16,256]{1,0:T(8,128)} fusion(f32[1,16,256]{2,1,0:T(8,128)S(1)} %collective-permute-done.4, f32[2,16,256]{2,1,0:T(8,128)S(1)} %bitcast_add_fusion.2, s32[]{:T(128)S(6)} %select_n.71), kind=kLoop, calls=%fused_computation.6 | loop fusion | flops 4096 | bytes 49156 | tf_op jit(solution)/shard_map/reshape | solution.py:253
  (7 shorter events, 0.1 us)
Async XLA Ops:
  0.0 5.1 %copy-start.3 = (s32[1,4]{1,0:T(1,128)S(1)}, s32[1,4]{1,0:T(1,128)}, u32[]{:S(2)}) copy-start(s32[1,4]{1,0:T(1,128)} %refs_3_.1) | copy-start | bytes 52
  0.0 5.1 %copy-start.5 = (bf16[16]{0:T(256)(128)(2,1)S(1)}, bf16[16]{0:T(256)(128)(2,1)}, u32[]{:S(2)}) copy-start(bf16[16]{0:T(256)(128)(2,1)} %param.8) | copy-start | bytes 100
  0.0 0.9 %copy-start = (s32[16,1024]{1,0:T(8,128)S(1)}, s32[16,1024]{1,0:T(8,128)}, u32[]{:S(2)}) copy-start(s32[16,1024]{1,0:T(8,128)} %refs_2_.5) | copy-start | bytes 196612
  0.9 0.7 %copy-start.2 = (s32[1,4]{1,0:T(1,128)S(1)}, s32[1,4]{1,0:T(1,128)}, u32[]{:S(2)}) copy-start(s32[1,4]{1,0:T(1,128)} %refs_3_.1) | copy-start | bytes 52
  1.5 0.7 %copy-start.4 = (bf16[16]{0:T(256)(128)(2,1)S(1)}, bf16[16]{0:T(256)(128)(2,1)}, u32[]{:S(2)}) copy-start(bf16[16]{0:T(256)(128)(2,1)} %param.8) | copy-start | bytes 100
  2.2 2.9 %copy-start.1 = (s32[16,1024]{1,0:T(8,128)S(1)}, s32[16,1024]{1,0:T(8,128)}, u32[]{:S(2)}) copy-start(s32[16,1024]{1,0:T(8,128)} %refs_2_.5) | copy-start | bytes 196612
  2.2 3.0 %copy-start.6 = (bf16[512,256]{1,0:T(8,128)(2,1)S(1)}, bf16[512,256]{1,0:T(8,128)(2,1)}, u32[]{:S(2)}) copy-start(bf16[512,256]{1,0:T(8,128)(2,1)} %constant.99.clone.refs_4_.refs_5_) | copy-start | bytes 786436
  3.8 11.9 %collective-permute-start = (bf16[1040,256]{1,0:T(8,128)(2,1)S(1)}, bf16[1040,256]{1,0:T(8,128)(2,1)S(1)}, u32[]{:S(2)}, u32[]{:S(2)}) collective-permute-start(bf16[1040,256]{1,0:T(8,128)(2,1)S(1)} %pack.1), channel_id=1, source_target_pairs={{1,0},{2,1},{3,2},{4,3},{5,4},{6,5},{7,6},{8,7},{9,8},{10,9},{11,1... | collective-permute-start | bytes 1597448 | tf_op jit(solution)/shard_map/ppermute | solution.py:279
  17.8 2.2 %collective-permute-start.1 = (f32[8,16,256]{2,1,0:T(8,128)S(1)}, f32[8,16,256]{2,1,0:T(8,128)S(1)}, u32[]{:S(2)}, u32[]{:S(2)}) collective-permute-start(f32[8,16,256]{2,1,0:T(8,128)S(1)} %dynamic-slice_bitcast_fusion), channel_id=1, source_target_pairs={{0,1},{1,0},{2,3},{3,2},{4,5},{5,4},{6,7},{7,6},{8,9},{9,8},{10,11... | collective-permute-start | bytes 393224 | tf_op jit(solution)/shard_map/ppermute | solution.py:251
  20.0 5.7 %collective-permute-start.2 = (f32[4,16,256]{2,1,0:T(8,128)S(1)}, f32[4,16,256]{2,1,0:T(8,128)S(1)}, u32[]{:S(2)}, u32[]{:S(2)}) collective-permute-start(f32[4,16,256]{2,1,0:T(8,128)S(1)} %dynamic-slice_bitcast_fusion.1), channel_id=1, source_target_pairs={{0,2},{1,3},{2,0},{3,1},{4,6},{5,7},{6,4},{7,5},{8,10},{9,11},{10,... | collective-permute-start | bytes 196616 | tf_op jit(solution)/shard_map/ppermute | solution.py:251
  25.7 4.4 %collective-permute-start.3 = (f32[2,16,256]{2,1,0:T(8,128)S(1)}, f32[2,16,256]{2,1,0:T(8,128)S(1)}, u32[]{:S(2)}, u32[]{:S(2)}) collective-permute-start(f32[2,16,256]{2,1,0:T(8,128)S(1)} %dynamic-slice_bitcast_fusion.2), channel_id=1, source_target_pairs={{0,4},{1,5},{2,6},{3,7},{4,0},{5,1},{6,2},{7,3},{8,12},{9,13},{10,... | collective-permute-start | bytes 98312 | tf_op jit(solution)/shard_map/ppermute | solution.py:251
  30.0 4.8 %collective-permute-start.4 = (f32[1,16,256]{2,1,0:T(8,128)S(1)}, f32[1,16,256]{2,1,0:T(8,128)S(1)}, u32[]{:S(2)}, u32[]{:S(2)}) collective-permute-start(f32[1,16,256]{2,1,0:T(8,128)S(1)} %constant_dynamic-slice_fusion), channel_id=1, source_target_pairs={{0,8},{1,9},{2,10},{3,11},{4,12},{5,13},{6,14},{7,15},{8,0},{9,1},... | collective-permute-start | bytes 49160 | tf_op jit(solution)/shard_map/ppermute | solution.py:251

commit v4 on v3

--- a/solution.py
+++ b/solution.py
@@ -62,20 +62,37 @@
 
 
 def pack_kernel(
-    rows_y, rows_x, snapshots_ref, material_ref, occupied_ref, moduli_ref, out_ref, rows, sem
+    rows_y, rows_x,
+    snapshots_ref, material_hbm, occupied_hbm, moduli_hbm,
+    out_ref,
+    material_ref, occupied_ref, moduli_ref, plane_ref, rows, sems,
 ):
     lanes, width = snapshots_ref.shape[1:]
-    plane = pltpu.make_async_copy(snapshots_ref.at[0], out_ref.at[pl.ds(0, lanes)], sem)
-    plane.start()
+    copies = [
+        pltpu.make_async_copy(source, target, sems.at[number])
+        for number, (source, target) in enumerate((
+            (material_hbm.at[pl.ds(0, 8)], material_ref),
+            (occupied_hbm, occupied_ref),
+            (moduli_hbm, moduli_ref),
+            (snapshots_ref.at[0], plane_ref.at[pl.ds(0, lanes)]),
+        ))
+    ]
+    for copy in copies:
+        copy.start()
+    for copy in copies[:3]:
+        copy.wait()
     occupied = lambda t: occupied_ref[0, t]
     place_y, place_x = lane_place((8, lanes), rows_x)
-    value = look_up(material_ref[:8, :], moduli_ref[...].astype(F32))
+    value = look_up(material_ref[...], moduli_ref[...].astype(F32))
     value = value * brick_select(occupied, rows_y, rows_x, place_y, place_x)
     rows[...] = jnp.zeros_like(rows)
     for part in range(lanes // width):
         rows[part : part + 1, :] = value[0:1, part * width : (part + 1) * width]
-    out_ref[lanes : lanes + 16, :] = rows[...].astype(BF16)
-    plane.wait()
+    plane_ref[lanes : lanes + 16, :] = rows[...].astype(BF16)
+    copies[3].wait()
+    send = pltpu.make_async_copy(plane_ref, out_ref, sems.at[4])
+    send.start()
+    send.wait()
 
 
 def main_kernel(
@@ -268,11 +285,18 @@
 
     packed = pl.pallas_call(
         lambda *refs: pack_kernel(rows_y, rows_x, *refs),
-        in_specs=[hbm, vmem, smem, vmem],
-        out_specs=vmem,
+        in_specs=[hbm, hbm, hbm, hbm],
+        out_specs=hbm,
         out_shape=jax.ShapeDtypeStruct((lanes + 16, width), BF16),
-        scratch_shapes=[pltpu.VMEM((16, width), F32), pltpu.SemaphoreType.DMA(())],
-        compiler_params=pltpu.CompilerParams(vmem_limit_bytes=52 << 20),
+        scratch_shapes=[
+            pltpu.VMEM((8, lanes), material.dtype),
+            pltpu.SMEM(occupancy.shape, occupancy.dtype),
+            pltpu.VMEM(moduli.shape, moduli.dtype),
+            pltpu.VMEM((lanes + 16, width), BF16),
+            pltpu.VMEM((16, width), F32),
+            pltpu.SemaphoreType.DMA((5,)),
+        ],
+        compiler_params=pltpu.CompilerParams(vmem_limit_bytes=56 << 20),
         name="pack",
     )(planes, material, occupancy, moduli)
 

time: 35.7 us -> 33.8 us (0.947)
  local copies, waits for them, and re-layouts: 2.24 us -> 0.06 us
  Pallas kernels: 14.1 us -> 14.5 us
    unnamed x14 -> x8, local copies, waits for them, and re-layouts: 2.19 us -> 0.01 us
    pallas_call x1, Pallas kernels: 1.59 us -> 1.96 us  [local(): pl.pallas_call(lambda *refs: pack_kernel(rows_y, rows_x, *refs), in_specs...]
  transfers between devices with their start and end apart: 5 -> 5, of which waited for: 4 -> 4; matrix products, arithmetic and copies ran while one was open for 0% -> 0% of each run, Pallas kernels for 30% -> 31%
where the time goes in v4:
time: 33.8 us; the launch traced here: 33.6 us
  Pallas kernels  14.5 us (43%)
  starting transfers between devices  11.1 us (33%)
  waiting for transfers between devices  7.21 us (21%)
  other arithmetic  0.64 us (2%)
    pallas_call x1, Pallas kernels, local(): pl.pallas_call(lambda *refs: main_kernel(rows_y, rows_x, *refs), in_specs...  10.6 us
    ppermute x4, starting transfers between devices, scatter_sum(): value = keep + lax.ppermute(give, axis, swap)  9.82 us
    ppermute x4, waiting for transfers between devices, scatter_sum(): value = keep + lax.ppermute(give, axis, swap)  7.2 us
    pallas_call x1, Pallas kernels, local(): pl.pallas_call(lambda *refs: pack_kernel(rows_y, rows_x, *refs), in_specs...  1.96 us
    pallas_call x1, Pallas kernels, local(): pl.pallas_call(lambda *refs: edge_kernel(rows_y, rows_x, scale, *refs), i...  1.96 us
    ppermute x1, starting transfers between devices, local(): lax.ppermute(packed, 'bricks', [(i + 1, i) for i in range(owners - 1)])  1.29 us
  transfers between devices with their start and end apart: 5, of which 4 were waited for; matrix products, arithmetic and copies ran while one was open for 0% of the time, Pallas kernels for 31%

profile of v4, /device:TPU:0, one launch (start us, length us, event | category | flops | bytes accessed | tf_op | source)
XLA Modules:
  0.0 33.6 jit_solution(11638516845072207962)
XLA Ops:
  0.0 0.0 copy-start.3
  0.0 0.0 copy-start.1
  0.0 0.0 copy-start
  0.0 0.0 copy-start.2
  0.0 2.0 %pack.1 = bf16[1040,256]{1,0:T(8,128)(2,1)} custom-call(bf16[16,1024,256]{2,1,0:T(8,128)(2,1)} %bitcast.24, s32[16,1024]{1,0:T(8,128)} %refs_2_.5, s32[1,4]{1,0:T(1,128)} %refs_3_.1, bf16[1,16]{1,0:T(2,128)(2,1)} %bitcast.21), custom_call_target="tpu_custom_call" | custom-call | tf_op jit(solution)/shard_map/pack/pallas_call | solution.py:286
  2.0 1.3 %collective-permute-start = (bf16[1040,256]{1,0:T(8,128)(2,1)}, bf16[1040,256]{1,0:T(8,128)(2,1)S(1)}, u32[]{:S(2)}, u32[]{:S(2)}) collective-permute-start(bf16[1040,256]{1,0:T(8,128)(2,1)} %pack.1), channel_id=1, source_target_pairs={{1,0},{2,1},{3,2},{4,3},{5,4},{6,5},{7,6},{8,7},{9,8},{10,9},{11,1... | collective-permute-start | bytes 1597448 | tf_op jit(solution)/shard_map/ppermute | solution.py:303
  3.3 0.0 copy-done.3
  3.3 0.0 copy-done.1
  3.3 0.0 copy-done
  3.3 0.0 copy-done.2
  3.3 10.6 %interior.1 = (f32[256,256]{1,0:T(8,128)S(1)}, bf16[1024,256]{1,0:T(8,128)(2,1)S(1)}) custom-call(bf16[16,1024,256]{2,1,0:T(8,128)(2,1)} %bitcast.25, s32[16,1024]{1,0:T(8,128)S(1)} %copy-done, s32[1,4]{1,0:T(1,128)S(1)} %copy-done.1, bf16[1,16]{1,0:T(2,128)(2,1)S(1)} %bitcast.22, bf16[512,256]{1,0:T(8,128)(2,1)S(1)} %copy-done.3), custom_call_target="tpu_custom_call" | custom-call | flops 6442450944 | bytes 8388608 | tf_op jit(solution)/shard_map/interior/pallas_call | solution.py:305
  13.9 0.0 collective-permute-done.refs_1_
  13.9 2.0 %edge.1 = f32[256,256]{1,0:T(8,128)S(1)} custom-call(bf16[1024,256]{1,0:T(8,128)(2,1)S(1)} %get-tuple-element.7.refs_0_, bf16[1040,256]{1,0:T(8,128)(2,1)S(1)} %collective-permute-done.refs_1_, s32[16,1024]{1,0:T(8,128)S(1)} %copy-done, s32[1,4]{1,0:T(1,128)S(1)} %copy-done.1, bf16[1,16]{1,0:T(2,128)(2,1)S(1)} %bitcast.23, bf16[512,256]{1,0:T(8,128)(2,1)S(1)} %copy-done.3, ...), custom_call_target="tpu_custom_call" | custom-call | flops 805306368 | bytes 1048576 | tf_op jit(solution)/shard_map/edge/pallas_call | solution.py:334
  15.9 1.2 %collective-permute-start.1 = (f32[8,16,256]{2,1,0:T(8,128)S(1)}, f32[8,16,256]{2,1,0:T(8,128)S(1)}, u32[]{:S(2)}, u32[]{:S(2)}) collective-permute-start(f32[8,16,256]{2,1,0:T(8,128)S(1)} %dynamic-slice_bitcast_fusion), channel_id=1, source_target_pairs={{0,1},{1,0},{2,3},{3,2},{4,5},{5,4},{6,7},{7,6},{8,9},{9,8},{10,11... | collective-permute-start | bytes 393224 | tf_op jit(solution)/shard_map/ppermute | solution.py:268
  17.1 1.0 %collective-permute-done.1 = f32[8,16,256]{2,1,0:T(8,128)S(1)} collective-permute-done((f32[8,16,256]{2,1,0:T(8,128)S(1)}, f32[8,16,256]{2,1,0:T(8,128)S(1)}, u32[]{:S(2)}, u32[]{:S(2)}) %collective-permute-start.1) | collective-permute-done | bytes 131104 | tf_op jit(solution)/shard_map/ppermute | solution.py:268
  18.1 3.1 %collective-permute-start.2 = (f32[4,16,256]{2,1,0:T(8,128)S(1)}, f32[4,16,256]{2,1,0:T(8,128)S(1)}, u32[]{:S(2)}, u32[]{:S(2)}) collective-permute-start(f32[4,16,256]{2,1,0:T(8,128)S(1)} %dynamic-slice_bitcast_fusion.1), channel_id=1, source_target_pairs={{0,2},{1,3},{2,0},{3,1},{4,6},{5,7},{6,4},{7,5},{8,10},{9,11},{10,... | collective-permute-start | bytes 196616 | tf_op jit(solution)/shard_map/ppermute | solution.py:268
  21.2 2.6 %collective-permute-done.2 = f32[4,16,256]{2,1,0:T(8,128)S(1)} collective-permute-done((f32[4,16,256]{2,1,0:T(8,128)S(1)}, f32[4,16,256]{2,1,0:T(8,128)S(1)}, u32[]{:S(2)}, u32[]{:S(2)}) %collective-permute-start.2) | collective-permute-done | bytes 65568 | tf_op jit(solution)/shard_map/ppermute | solution.py:268
  23.8 2.5 %collective-permute-start.3 = (f32[2,16,256]{2,1,0:T(8,128)S(1)}, f32[2,16,256]{2,1,0:T(8,128)S(1)}, u32[]{:S(2)}, u32[]{:S(2)}) collective-permute-start(f32[2,16,256]{2,1,0:T(8,128)S(1)} %dynamic-slice_bitcast_fusion.2), channel_id=1, source_target_pairs={{0,4},{1,5},{2,6},{3,7},{4,0},{5,1},{6,2},{7,3},{8,12},{9,13},{10,... | collective-permute-start | bytes 98312 | tf_op jit(solution)/shard_map/ppermute | solution.py:268
  26.3 1.9 %collective-permute-done.3 = f32[2,16,256]{2,1,0:T(8,128)S(1)} collective-permute-done((f32[2,16,256]{2,1,0:T(8,128)S(1)}, f32[2,16,256]{2,1,0:T(8,128)S(1)}, u32[]{:S(2)}, u32[]{:S(2)}) %collective-permute-start.3) | collective-permute-done | bytes 32800 | tf_op jit(solution)/shard_map/ppermute | solution.py:268
  28.2 3.1 %collective-permute-start.4 = (f32[1,16,256]{2,1,0:T(8,128)S(1)}, f32[1,16,256]{2,1,0:T(8,128)S(1)}, u32[]{:S(2)}, u32[]{:S(2)}) collective-permute-start(f32[1,16,256]{2,1,0:T(8,128)S(1)} %constant_dynamic-slice_fusion), channel_id=1, source_target_pairs={{0,8},{1,9},{2,10},{3,11},{4,12},{5,13},{6,14},{7,15},{8,0},{9,1},... | collective-permute-start | bytes 49160 | tf_op jit(solution)/shard_map/ppermute | solution.py:268
  31.3 1.7 %collective-permute-done.4 = f32[1,16,256]{2,1,0:T(8,128)S(1)} collective-permute-done((f32[1,16,256]{2,1,0:T(8,128)S(1)}, f32[1,16,256]{2,1,0:T(8,128)S(1)}, u32[]{:S(2)}, u32[]{:S(2)}) %collective-permute-start.4) | collective-permute-done | bytes 16416 | tf_op jit(solution)/shard_map/ppermute | solution.py:268
  33.0 0.6 %add_bitcast_fusion = f32[16,256]{1,0:T(8,128)} fusion(f32[1,16,256]{2,1,0:T(8,128)S(1)} %collective-permute-done.4, f32[2,16,256]{2,1,0:T(8,128)S(1)} %bitcast_add_fusion.2, s32[]{:T(128)S(6)} %select_n.71), kind=kLoop, calls=%fused_computation.6 | loop fusion | flops 4096 | bytes 49156 | tf_op jit(solution)/shard_map/reshape | solution.py:270
  (7 shorter events, 0.1 us)
Async XLA Ops:
  0.0 3.3 %copy-start.3 = (bf16[512,256]{1,0:T(8,128)(2,1)S(1)}, bf16[512,256]{1,0:T(8,128)(2,1)}, u32[]{:S(2)}) copy-start(bf16[512,256]{1,0:T(8,128)(2,1)} %constant.99.clone.refs_4_.refs_5_) | copy-start | bytes 786436
  0.0 3.3 %copy-start.1 = (s32[1,4]{1,0:T(1,128)S(1)}, s32[1,4]{1,0:T(1,128)}, u32[]{:S(2)}) copy-start(s32[1,4]{1,0:T(1,128)} %refs_3_.1) | copy-start | bytes 52
  0.0 3.3 %copy-start = (s32[16,1024]{1,0:T(8,128)S(1)}, s32[16,1024]{1,0:T(8,128)}, u32[]{:S(2)}) copy-start(s32[16,1024]{1,0:T(8,128)} %refs_2_.5) | copy-start | bytes 196612
  0.0 3.3 %copy-start.2 = (bf16[16]{0:T(256)(128)(2,1)S(1)}, bf16[16]{0:T(256)(128)(2,1)}, u32[]{:S(2)}) copy-start(bf16[16]{0:T(256)(128)(2,1)} %param.8) | copy-start | bytes 100
  2.0 11.9 %collective-permute-start = (bf16[1040,256]{1,0:T(8,128)(2,1)}, bf16[1040,256]{1,0:T(8,128)(2,1)S(1)}, u32[]{:S(2)}, u32[]{:S(2)}) collective-permute-start(bf16[1040,256]{1,0:T(8,128)(2,1)} %pack.1), channel_id=1, source_target_pairs={{1,0},{2,1},{3,2},{4,3},{5,4},{6,5},{7,6},{8,7},{9,8},{10,9},{11,1... | collective-permute-start | bytes 1597448 | tf_op jit(solution)/shard_map/ppermute | solution.py:303
  15.9 2.2 %collective-permute-start.1 = (f32[8,16,256]{2,1,0:T(8,128)S(1)}, f32[8,16,256]{2,1,0:T(8,128)S(1)}, u32[]{:S(2)}, u32[]{:S(2)}) collective-permute-start(f32[8,16,256]{2,1,0:T(8,128)S(1)} %dynamic-slice_bitcast_fusion), channel_id=1, source_target_pairs={{0,1},{1,0},{2,3},{3,2},{4,5},{5,4},{6,7},{7,6},{8,9},{9,8},{10,11... | collective-permute-start | bytes 393224 | tf_op jit(solution)/shard_map/ppermute | solution.py:268
  18.1 5.7 %collective-permute-start.2 = (f32[4,16,256]{2,1,0:T(8,128)S(1)}, f32[4,16,256]{2,1,0:T(8,128)S(1)}, u32[]{:S(2)}, u32[]{:S(2)}) collective-permute-start(f32[4,16,256]{2,1,0:T(8,128)S(1)} %dynamic-slice_bitcast_fusion.1), channel_id=1, source_target_pairs={{0,2},{1,3},{2,0},{3,1},{4,6},{5,7},{6,4},{7,5},{8,10},{9,11},{10,... | collective-permute-start | bytes 196616 | tf_op jit(solution)/shard_map/ppermute | solution.py:268
  23.8 4.4 %collective-permute-start.3 = (f32[2,16,256]{2,1,0:T(8,128)S(1)}, f32[2,16,256]{2,1,0:T(8,128)S(1)}, u32[]{:S(2)}, u32[]{:S(2)}) collective-permute-start(f32[2,16,256]{2,1,0:T(8,128)S(1)} %dynamic-slice_bitcast_fusion.2), channel_id=1, source_target_pairs={{0,4},{1,5},{2,6},{3,7},{4,0},{5,1},{6,2},{7,3},{8,12},{9,13},{10,... | collective-permute-start | bytes 98312 | tf_op jit(solution)/shard_map/ppermute | solution.py:268
  28.2 4.8 %collective-permute-start.4 = (f32[1,16,256]{2,1,0:T(8,128)S(1)}, f32[1,16,256]{2,1,0:T(8,128)S(1)}, u32[]{:S(2)}, u32[]{:S(2)}) collective-permute-start(f32[1,16,256]{2,1,0:T(8,128)S(1)} %constant_dynamic-slice_fusion), channel_id=1, source_target_pairs={{0,8},{1,9},{2,10},{3,11},{4,12},{5,13},{6,14},{7,15},{8,0},{9,1},... | collective-permute-start | bytes 49160 | tf_op jit(solution)/shard_map/ppermute | solution.py:268

commit v5 on v4

--- a/solution.py
+++ b/solution.py
@@ -99,7 +99,7 @@
     rows_y, rows_x,
     snapshots_ref, material_ref, occupied_ref, moduli_ref, weights_ref,
     out_ref, top_ref,
-    field, lhs, last, pair, image, modulus_rows, center_columns, masked, sems, top_sem,
+    field, field_t, lhs, last, pair, image, modulus_rows, center_columns, masked, sems, top_sem,
 ):
     depth, lanes, width = snapshots_ref.shape
     blocks = lanes // BLOCK
@@ -166,40 +166,45 @@
         sink(z, per_block * blocks - 1, above)
 
     def start(z, y, new):
-        rows = pl.ds(y * rows_x, rows_x)
-        last[rows, :] = new
-        pair[rows, :] = new
+        last[pl.ds(y * rows_x, rows_x), :] = new
+
+    def write_image(z, rows, both):
+        scale = jnp.broadcast_to(center_columns[rows, z : z + 1], (rows_x, width))
+        image[z % 2, rows, :] = (scale * field[z, rows, :].astype(F32) - both).astype(BF16)
 
     def emit(z, y, new):
         rows = pl.ds(y * rows_x, rows_x)
-        now = last[rows, :] if new is None else last[rows, :] + new
-        both = pair[rows, :] + now
-        scale = jnp.broadcast_to(center_columns[rows, z - 1 : z], (rows_x, width))
-        value = scale * field[z - 1, rows, :].astype(F32) - both
-        image[(z - 1) % 2, rows, :] = value.astype(BF16)
-        if new is not None:
+        old = last[rows, :]
+        now = old + new
+        write_image(z - 1, rows, (old if z == 1 else pair[rows, :]) + now)
+        if z == depth - 1:
+            write_image(z, rows, now + new)
+        else:
             last[rows, :] = new
             pair[rows, :] = now
 
+    def turn(z):
+        field_t[z % 2] = field[z].T
+
     def gram(z):
-        out_ref[...] += jnp.dot(image[z % 2].T, field[z], preferred_element_type=F32)
+        out_ref[...] += jnp.dot(field_t[z % 2], image[z % 2], preferred_element_type=F32)
 
     top = pltpu.make_async_copy(field.at[depth - 1], top_ref, top_sem)
-    copy(0).wait()
-    plane(0, start)
-    for z in range(1, depth + 1):
+    for z in range(depth):
+        if z == 0 or z % 5 == 2:
+            for ahead in range(z, min(z + 5 if z else 2, depth)):
+                copy(ahead).wait()
+                if ahead == depth - 1:
+                    top.start()
+        if z == 0:
+            plane(z, start)
+            continue
         if z >= 2:
             gram(z - 2)
-        if z < depth:
-            if (z - 1) % 3 == 0:
-                for ahead in range(z, min(z + 3, depth)):
-                    copy(ahead).wait()
-                    if ahead == depth - 1:
-                        top.start()
-            plane(z, emit)
-        else:
-            for y in range(rows_y):
-                emit(z, y, None)
+        turn(z - 1)
+        plane(z, emit)
+    gram(depth - 2)
+    turn(depth - 1)
     gram(depth - 1)
     top.wait()
 
@@ -312,6 +317,7 @@
         ),
         scratch_shapes=[
             pltpu.VMEM((depth, lanes, width), BF16),
+            pltpu.VMEM((2, width, lanes), BF16),
             pltpu.VMEM((2, reach, BLOCK), BF16),
             pltpu.VMEM((lanes, width), F32),
             pltpu.VMEM((lanes, width), F32),

time: 33.8 us -> 33.5 us (level)
  no operation moved by 1% of the time
where the time goes in v5:
time: 33.5 us; the launch traced here: 33.3 us
  Pallas kernels  14.2 us (42%)
  starting transfers between devices  11.1 us (33%)
  waiting for transfers between devices  7.21 us (22%)
  other arithmetic  0.64 us (2%)
    pallas_call x1, Pallas kernels, local(): pl.pallas_call(lambda *refs: main_kernel(rows_y, rows_x, *refs), in_specs...  10.3 us
    ppermute x4, starting transfers between devices, scatter_sum(): value = keep + lax.ppermute(give, axis, swap)  9.81 us
    ppermute x4, waiting for transfers between devices, scatter_sum(): value = keep + lax.ppermute(give, axis, swap)  7.2 us
    pallas_call x1, Pallas kernels, local(): pl.pallas_call(lambda *refs: pack_kernel(rows_y, rows_x, *refs), in_specs...  1.96 us
    pallas_call x1, Pallas kernels, local(): pl.pallas_call(lambda *refs: edge_kernel(rows_y, rows_x, scale, *refs), i...  1.96 us
    ppermute x1, starting transfers between devices, local(): lax.ppermute(packed, 'bricks', [(i + 1, i) for i in range(owners - 1)])  1.29 us
  transfers between devices with their start and end apart: 5, of which 4 were waited for; matrix products, arithmetic and copies ran while one was open for 0% of the time, Pallas kernels for 31%

profile of v5, /device:TPU:0, one launch (start us, length us, event | category | flops | bytes accessed | tf_op | source)
XLA Modules:
  0.0 33.3 jit_solution(239045926642608300)
XLA Ops:
  0.0 0.0 copy-start.3
  0.0 0.0 copy-start.1
  0.0 0.0 copy-start
  0.0 0.0 copy-start.2
  0.0 2.0 %pack.1 = bf16[1040,256]{1,0:T(8,128)(2,1)} custom-call(bf16[16,1024,256]{2,1,0:T(8,128)(2,1)} %bitcast.24, s32[16,1024]{1,0:T(8,128)} %refs_2_.5, s32[1,4]{1,0:T(1,128)} %refs_3_.1, bf16[1,16]{1,0:T(2,128)(2,1)} %bitcast.21), custom_call_target="tpu_custom_call" | custom-call | tf_op jit(solution)/shard_map/pack/pallas_call | solution.py:291
  2.0 1.3 %collective-permute-start = (bf16[1040,256]{1,0:T(8,128)(2,1)}, bf16[1040,256]{1,0:T(8,128)(2,1)S(1)}, u32[]{:S(2)}, u32[]{:S(2)}) collective-permute-start(bf16[1040,256]{1,0:T(8,128)(2,1)} %pack.1), channel_id=1, source_target_pairs={{1,0},{2,1},{3,2},{4,3},{5,4},{6,5},{7,6},{8,7},{9,8},{10,9},{11,1... | collective-permute-start | bytes 1597448 | tf_op jit(solution)/shard_map/ppermute | solution.py:308
  3.3 0.0 copy-done.3
  3.3 0.0 copy-done.1
  3.3 0.0 copy-done
  3.3 0.0 copy-done.2
  3.3 10.3 %interior.1 = (f32[256,256]{1,0:T(8,128)S(1)}, bf16[1024,256]{1,0:T(8,128)(2,1)S(1)}) custom-call(bf16[16,1024,256]{2,1,0:T(8,128)(2,1)} %bitcast.25, s32[16,1024]{1,0:T(8,128)S(1)} %copy-done, s32[1,4]{1,0:T(1,128)S(1)} %copy-done.1, bf16[1,16]{1,0:T(2,128)(2,1)S(1)} %bitcast.22, bf16[512,256]{1,0:T(8,128)(2,1)S(1)} %copy-done.3), custom_call_target="tpu_custom_call" | custom-call | flops 6442450944 | bytes 8388608 | tf_op jit(solution)/shard_map/interior/pallas_call | solution.py:310
  13.6 0.0 collective-permute-done.refs_1_
  13.6 2.0 %edge.1 = f32[256,256]{1,0:T(8,128)S(1)} custom-call(bf16[1024,256]{1,0:T(8,128)(2,1)S(1)} %get-tuple-element.7.refs_0_, bf16[1040,256]{1,0:T(8,128)(2,1)S(1)} %collective-permute-done.refs_1_, s32[16,1024]{1,0:T(8,128)S(1)} %copy-done, s32[1,4]{1,0:T(1,128)S(1)} %copy-done.1, bf16[1,16]{1,0:T(2,128)(2,1)S(1)} %bitcast.23, bf16[512,256]{1,0:T(8,128)(2,1)S(1)} %copy-done.3, ...), custom_call_target="tpu_custom_call" | custom-call | flops 805306368 | bytes 1048576 | tf_op jit(solution)/shard_map/edge/pallas_call | solution.py:340
  15.6 1.2 %collective-permute-start.1 = (f32[8,16,256]{2,1,0:T(8,128)S(1)}, f32[8,16,256]{2,1,0:T(8,128)S(1)}, u32[]{:S(2)}, u32[]{:S(2)}) collective-permute-start(f32[8,16,256]{2,1,0:T(8,128)S(1)} %dynamic-slice_bitcast_fusion), channel_id=1, source_target_pairs={{0,1},{1,0},{2,3},{3,2},{4,5},{5,4},{6,7},{7,6},{8,9},{9,8},{10,11... | collective-permute-start | bytes 393224 | tf_op jit(solution)/shard_map/ppermute | solution.py:273
  16.8 1.0 %collective-permute-done.1 = f32[8,16,256]{2,1,0:T(8,128)S(1)} collective-permute-done((f32[8,16,256]{2,1,0:T(8,128)S(1)}, f32[8,16,256]{2,1,0:T(8,128)S(1)}, u32[]{:S(2)}, u32[]{:S(2)}) %collective-permute-start.1) | collective-permute-done | bytes 131104 | tf_op jit(solution)/shard_map/ppermute | solution.py:273
  17.8 3.1 %collective-permute-start.2 = (f32[4,16,256]{2,1,0:T(8,128)S(1)}, f32[4,16,256]{2,1,0:T(8,128)S(1)}, u32[]{:S(2)}, u32[]{:S(2)}) collective-permute-start(f32[4,16,256]{2,1,0:T(8,128)S(1)} %dynamic-slice_bitcast_fusion.1), channel_id=1, source_target_pairs={{0,2},{1,3},{2,0},{3,1},{4,6},{5,7},{6,4},{7,5},{8,10},{9,11},{10,... | collective-permute-start | bytes 196616 | tf_op jit(solution)/shard_map/ppermute | solution.py:273
  20.9 2.6 %collective-permute-done.2 = f32[4,16,256]{2,1,0:T(8,128)S(1)} collective-permute-done((f32[4,16,256]{2,1,0:T(8,128)S(1)}, f32[4,16,256]{2,1,0:T(8,128)S(1)}, u32[]{:S(2)}, u32[]{:S(2)}) %collective-permute-start.2) | collective-permute-done | bytes 65568 | tf_op jit(solution)/shard_map/ppermute | solution.py:273
  23.5 2.5 %collective-permute-start.3 = (f32[2,16,256]{2,1,0:T(8,128)S(1)}, f32[2,16,256]{2,1,0:T(8,128)S(1)}, u32[]{:S(2)}, u32[]{:S(2)}) collective-permute-start(f32[2,16,256]{2,1,0:T(8,128)S(1)} %dynamic-slice_bitcast_fusion.2), channel_id=1, source_target_pairs={{0,4},{1,5},{2,6},{3,7},{4,0},{5,1},{6,2},{7,3},{8,12},{9,13},{10,... | collective-permute-start | bytes 98312 | tf_op jit(solution)/shard_map/ppermute | solution.py:273
  26.0 1.9 %collective-permute-done.3 = f32[2,16,256]{2,1,0:T(8,128)S(1)} collective-permute-done((f32[2,16,256]{2,1,0:T(8,128)S(1)}, f32[2,16,256]{2,1,0:T(8,128)S(1)}, u32[]{:S(2)}, u32[]{:S(2)}) %collective-permute-start.3) | collective-permute-done | bytes 32800 | tf_op jit(solution)/shard_map/ppermute | solution.py:273
  27.9 3.1 %collective-permute-start.4 = (f32[1,16,256]{2,1,0:T(8,128)S(1)}, f32[1,16,256]{2,1,0:T(8,128)S(1)}, u32[]{:S(2)}, u32[]{:S(2)}) collective-permute-start(f32[1,16,256]{2,1,0:T(8,128)S(1)} %constant_dynamic-slice_fusion), channel_id=1, source_target_pairs={{0,8},{1,9},{2,10},{3,11},{4,12},{5,13},{6,14},{7,15},{8,0},{9,1},... | collective-permute-start | bytes 49160 | tf_op jit(solution)/shard_map/ppermute | solution.py:273
  31.0 1.7 %collective-permute-done.4 = f32[1,16,256]{2,1,0:T(8,128)S(1)} collective-permute-done((f32[1,16,256]{2,1,0:T(8,128)S(1)}, f32[1,16,256]{2,1,0:T(8,128)S(1)}, u32[]{:S(2)}, u32[]{:S(2)}) %collective-permute-start.4) | collective-permute-done | bytes 16416 | tf_op jit(solution)/shard_map/ppermute | solution.py:273
  32.7 0.6 %add_bitcast_fusion = f32[16,256]{1,0:T(8,128)} fusion(f32[1,16,256]{2,1,0:T(8,128)S(1)} %collective-permute-done.4, f32[2,16,256]{2,1,0:T(8,128)S(1)} %bitcast_add_fusion.2, s32[]{:T(128)S(6)} %select_n.71), kind=kLoop, calls=%fused_computation.6 | loop fusion | flops 4096 | bytes 49156 | tf_op jit(solution)/shard_map/reshape | solution.py:275
  (7 shorter events, 0.1 us)
Async XLA Ops:
  0.0 3.3 %copy-start.3 = (bf16[512,256]{1,0:T(8,128)(2,1)S(1)}, bf16[512,256]{1,0:T(8,128)(2,1)}, u32[]{:S(2)}) copy-start(bf16[512,256]{1,0:T(8,128)(2,1)} %constant.99.clone.refs_4_.refs_5_) | copy-start | bytes 786436
  0.0 3.3 %copy-start.1 = (s32[1,4]{1,0:T(1,128)S(1)}, s32[1,4]{1,0:T(1,128)}, u32[]{:S(2)}) copy-start(s32[1,4]{1,0:T(1,128)} %refs_3_.1) | copy-start | bytes 52
  0.0 3.3 %copy-start = (s32[16,1024]{1,0:T(8,128)S(1)}, s32[16,1024]{1,0:T(8,128)}, u32[]{:S(2)}) copy-start(s32[16,1024]{1,0:T(8,128)} %refs_2_.5) | copy-start | bytes 196612
  0.0 3.3 %copy-start.2 = (bf16[16]{0:T(256)(128)(2,1)S(1)}, bf16[16]{0:T(256)(128)(2,1)}, u32[]{:S(2)}) copy-start(bf16[16]{0:T(256)(128)(2,1)} %param.8) | copy-start | bytes 100
  2.0 11.6 %collective-permute-start = (bf16[1040,256]{1,0:T(8,128)(2,1)}, bf16[1040,256]{1,0:T(8,128)(2,1)S(1)}, u32[]{:S(2)}, u32[]{:S(2)}) collective-permute-start(bf16[1040,256]{1,0:T(8,128)(2,1)} %pack.1), channel_id=1, source_target_pairs={{1,0},{2,1},{3,2},{4,3},{5,4},{6,5},{7,6},{8,7},{9,8},{10,9},{11,1... | collective-permute-start | bytes 1597448 | tf_op jit(solution)/shard_map/ppermute | solution.py:308
  15.6 2.2 %collective-permute-start.1 = (f32[8,16,256]{2,1,0:T(8,128)S(1)}, f32[8,16,256]{2,1,0:T(8,128)S(1)}, u32[]{:S(2)}, u32[]{:S(2)}) collective-permute-start(f32[8,16,256]{2,1,0:T(8,128)S(1)} %dynamic-slice_bitcast_fusion), channel_id=1, source_target_pairs={{0,1},{1,0},{2,3},{3,2},{4,5},{5,4},{6,7},{7,6},{8,9},{9,8},{10,11... | collective-permute-start | bytes 393224 | tf_op jit(solution)/shard_map/ppermute | solution.py:273
  17.8 5.7 %collective-permute-start.2 = (f32[4,16,256]{2,1,0:T(8,128)S(1)}, f32[4,16,256]{2,1,0:T(8,128)S(1)}, u32[]{:S(2)}, u32[]{:S(2)}) collective-permute-start(f32[4,16,256]{2,1,0:T(8,128)S(1)} %dynamic-slice_bitcast_fusion.1), channel_id=1, source_target_pairs={{0,2},{1,3},{2,0},{3,1},{4,6},{5,7},{6,4},{7,5},{8,10},{9,11},{10,... | collective-permute-start | bytes 196616 | tf_op jit(solution)/shard_map/ppermute | solution.py:273
  23.5 4.4 %collective-permute-start.3 = (f32[2,16,256]{2,1,0:T(8,128)S(1)}, f32[2,16,256]{2,1,0:T(8,128)S(1)}, u32[]{:S(2)}, u32[]{:S(2)}) collective-permute-start(f32[2,16,256]{2,1,0:T(8,128)S(1)} %dynamic-slice_bitcast_fusion.2), channel_id=1, source_target_pairs={{0,4},{1,5},{2,6},{3,7},{4,0},{5,1},{6,2},{7,3},{8,12},{9,13},{10,... | collective-permute-start | bytes 98312 | tf_op jit(solution)/shard_map/ppermute | solution.py:273
  27.9 4.8 %collective-permute-start.4 = (f32[1,16,256]{2,1,0:T(8,128)S(1)}, f32[1,16,256]{2,1,0:T(8,128)S(1)}, u32[]{:S(2)}, u32[]{:S(2)}) collective-permute-start(f32[1,16,256]{2,1,0:T(8,128)S(1)} %constant_dynamic-slice_fusion), channel_id=1, source_target_pairs={{0,8},{1,9},{2,10},{3,11},{4,12},{5,13},{6,14},{7,15},{8,0},{9,1},... | collective-permute-start | bytes 49160 | tf_op jit(solution)/shard_map/ppermute | solution.py:273

commit v6 on v5

--- a/solution.py
+++ b/solution.py
@@ -68,18 +68,32 @@
     material_ref, occupied_ref, moduli_ref, plane_ref, rows, sems,
 ):
     lanes, width = snapshots_ref.shape[1:]
+    parts = 4
+    size = lanes // parts
     copies = [
         pltpu.make_async_copy(source, target, sems.at[number])
         for number, (source, target) in enumerate((
             (material_hbm.at[pl.ds(0, 8)], material_ref),
             (occupied_hbm, occupied_ref),
             (moduli_hbm, moduli_ref),
-            (snapshots_ref.at[0], plane_ref.at[pl.ds(0, lanes)]),
         ))
     ]
+    pieces = [pl.ds(part * size, size) for part in range(parts)]
+    loads = [
+        pltpu.make_async_copy(snapshots_ref.at[0, piece], plane_ref.at[piece], sems.at[3 + number])
+        for number, piece in enumerate(pieces)
+    ]
+    for copy in copies + loads:
+        copy.start()
+    pieces.append(pl.ds(lanes, 16))
+    sends = [
+        pltpu.make_async_copy(plane_ref.at[piece], out_ref.at[piece], sems.at[3 + parts + number])
+        for number, piece in enumerate(pieces)
+    ]
+    for load, send in zip(loads, sends):
+        load.wait()
+        send.start()
     for copy in copies:
-        copy.start()
-    for copy in copies[:3]:
         copy.wait()
     occupied = lambda t: occupied_ref[0, t]
     place_y, place_x = lane_place((8, lanes), rows_x)
@@ -89,10 +103,9 @@
     for part in range(lanes // width):
         rows[part : part + 1, :] = value[0:1, part * width : (part + 1) * width]
     plane_ref[lanes : lanes + 16, :] = rows[...].astype(BF16)
-    copies[3].wait()
-    send = pltpu.make_async_copy(plane_ref, out_ref, sems.at[4])
-    send.start()
-    send.wait()
+    sends[-1].start()
+    for send in sends:
+        send.wait()
 
 
 def main_kernel(
@@ -299,7 +312,7 @@
             pltpu.VMEM(moduli.shape, moduli.dtype),
             pltpu.VMEM((lanes + 16, width), BF16),
             pltpu.VMEM((16, width), F32),
-            pltpu.SemaphoreType.DMA((5,)),
+            pltpu.SemaphoreType.DMA((12,)),
         ],
         compiler_params=pltpu.CompilerParams(vmem_limit_bytes=56 << 20),
         name="pack",

time: 33.5 us -> 33.6 us (level)
  no operation moved by 1% of the time
where the time goes in v6:
time: 33.6 us; the launch traced here: 33.4 us
  Pallas kernels  14.3 us (43%)
  starting transfers between devices  11.1 us (33%)
  waiting for transfers between devices  7.21 us (21%)
  other arithmetic  0.64 us (2%)
    pallas_call x1, Pallas kernels, local(): pl.pallas_call(lambda *refs: main_kernel(rows_y, rows_x, *refs), in_specs...  10.3 us
    ppermute x4, starting transfers between devices, scatter_sum(): value = keep + lax.ppermute(give, axis, swap)  9.82 us
    ppermute x4, waiting for transfers between devices, scatter_sum(): value = keep + lax.ppermute(give, axis, swap)  7.2 us
    pallas_call x1, Pallas kernels, local(): pl.pallas_call(lambda *refs: pack_kernel(rows_y, rows_x, *refs), in_specs...  2.06 us
    pallas_call x1, Pallas kernels, local(): pl.pallas_call(lambda *refs: edge_kernel(rows_y, rows_x, scale, *refs), i...  1.96 us
    ppermute x1, starting transfers between devices, local(): lax.ppermute(packed, 'bricks', [(i + 1, i) for i in range(owners - 1)])  1.29 us
  transfers between devices with their start and end apart: 5, of which 4 were waited for; matrix products, arithmetic and copies ran while one was open for 0% of the time, Pallas kernels for 31%

profile of v6, /device:TPU:0, one launch (start us, length us, event | category | flops | bytes accessed | tf_op | source)
XLA Modules:
  0.0 33.4 jit_solution(10926811018636375615)
XLA Ops:
  0.0 0.0 copy-start.3
  0.0 0.0 copy-start.1
  0.0 0.0 copy-start
  0.0 0.0 copy-start.2
  0.0 2.1 %pack.1 = bf16[1040,256]{1,0:T(8,128)(2,1)} custom-call(bf16[16,1024,256]{2,1,0:T(8,128)(2,1)} %bitcast.24, s32[16,1024]{1,0:T(8,128)} %refs_2_.5, s32[1,4]{1,0:T(1,128)} %refs_3_.1, bf16[1,16]{1,0:T(2,128)(2,1)} %bitcast.21), custom_call_target="tpu_custom_call" | custom-call | tf_op jit(solution)/shard_map/pack/pallas_call | solution.py:304
  2.1 1.3 %collective-permute-start = (bf16[1040,256]{1,0:T(8,128)(2,1)}, bf16[1040,256]{1,0:T(8,128)(2,1)S(1)}, u32[]{:S(2)}, u32[]{:S(2)}) collective-permute-start(bf16[1040,256]{1,0:T(8,128)(2,1)} %pack.1), channel_id=1, source_target_pairs={{1,0},{2,1},{3,2},{4,3},{5,4},{6,5},{7,6},{8,7},{9,8},{10,9},{11,1... | collective-permute-start | bytes 1597448 | tf_op jit(solution)/shard_map/ppermute | solution.py:321
  3.4 0.0 copy-done.3
  3.4 0.0 copy-done.1
  3.4 0.0 copy-done
  3.4 0.0 copy-done.2
  3.4 10.3 %interior.1 = (f32[256,256]{1,0:T(8,128)S(1)}, bf16[1024,256]{1,0:T(8,128)(2,1)S(1)}) custom-call(bf16[16,1024,256]{2,1,0:T(8,128)(2,1)} %bitcast.25, s32[16,1024]{1,0:T(8,128)S(1)} %copy-done, s32[1,4]{1,0:T(1,128)S(1)} %copy-done.1, bf16[1,16]{1,0:T(2,128)(2,1)S(1)} %bitcast.22, bf16[512,256]{1,0:T(8,128)(2,1)S(1)} %copy-done.3), custom_call_target="tpu_custom_call" | custom-call | flops 6442450944 | bytes 8388608 | tf_op jit(solution)/shard_map/interior/pallas_call | solution.py:323
  13.7 0.0 collective-permute-done.refs_1_
  13.7 2.0 %edge.1 = f32[256,256]{1,0:T(8,128)S(1)} custom-call(bf16[1024,256]{1,0:T(8,128)(2,1)S(1)} %get-tuple-element.7.refs_0_, bf16[1040,256]{1,0:T(8,128)(2,1)S(1)} %collective-permute-done.refs_1_, s32[16,1024]{1,0:T(8,128)S(1)} %copy-done, s32[1,4]{1,0:T(1,128)S(1)} %copy-done.1, bf16[1,16]{1,0:T(2,128)(2,1)S(1)} %bitcast.23, bf16[512,256]{1,0:T(8,128)(2,1)S(1)} %copy-done.3, ...), custom_call_target="tpu_custom_call" | custom-call | flops 805306368 | bytes 1048576 | tf_op jit(solution)/shard_map/edge/pallas_call | solution.py:353
  15.7 1.2 %collective-permute-start.1 = (f32[8,16,256]{2,1,0:T(8,128)S(1)}, f32[8,16,256]{2,1,0:T(8,128)S(1)}, u32[]{:S(2)}, u32[]{:S(2)}) collective-permute-start(f32[8,16,256]{2,1,0:T(8,128)S(1)} %dynamic-slice_bitcast_fusion), channel_id=1, source_target_pairs={{0,1},{1,0},{2,3},{3,2},{4,5},{5,4},{6,7},{7,6},{8,9},{9,8},{10,11... | collective-permute-start | bytes 393224 | tf_op jit(solution)/shard_map/ppermute | solution.py:286
  16.9 1.0 %collective-permute-done.1 = f32[8,16,256]{2,1,0:T(8,128)S(1)} collective-permute-done((f32[8,16,256]{2,1,0:T(8,128)S(1)}, f32[8,16,256]{2,1,0:T(8,128)S(1)}, u32[]{:S(2)}, u32[]{:S(2)}) %collective-permute-start.1) | collective-permute-done | bytes 131104 | tf_op jit(solution)/shard_map/ppermute | solution.py:286
  17.9 3.1 %collective-permute-start.2 = (f32[4,16,256]{2,1,0:T(8,128)S(1)}, f32[4,16,256]{2,1,0:T(8,128)S(1)}, u32[]{:S(2)}, u32[]{:S(2)}) collective-permute-start(f32[4,16,256]{2,1,0:T(8,128)S(1)} %dynamic-slice_bitcast_fusion.1), channel_id=1, source_target_pairs={{0,2},{1,3},{2,0},{3,1},{4,6},{5,7},{6,4},{7,5},{8,10},{9,11},{10,... | collective-permute-start | bytes 196616 | tf_op jit(solution)/shard_map/ppermute | solution.py:286
  21.0 2.6 %collective-permute-done.2 = f32[4,16,256]{2,1,0:T(8,128)S(1)} collective-permute-done((f32[4,16,256]{2,1,0:T(8,128)S(1)}, f32[4,16,256]{2,1,0:T(8,128)S(1)}, u32[]{:S(2)}, u32[]{:S(2)}) %collective-permute-start.2) | collective-permute-done | bytes 65568 | tf_op jit(solution)/shard_map/ppermute | solution.py:286
  23.6 2.5 %collective-permute-start.3 = (f32[2,16,256]{2,1,0:T(8,128)S(1)}, f32[2,16,256]{2,1,0:T(8,128)S(1)}, u32[]{:S(2)}, u32[]{:S(2)}) collective-permute-start(f32[2,16,256]{2,1,0:T(8,128)S(1)} %dynamic-slice_bitcast_fusion.2), channel_id=1, source_target_pairs={{0,4},{1,5},{2,6},{3,7},{4,0},{5,1},{6,2},{7,3},{8,12},{9,13},{10,... | collective-permute-start | bytes 98312 | tf_op jit(solution)/shard_map/ppermute | solution.py:286
  26.1 1.9 %collective-permute-done.3 = f32[2,16,256]{2,1,0:T(8,128)S(1)} collective-permute-done((f32[2,16,256]{2,1,0:T(8,128)S(1)}, f32[2,16,256]{2,1,0:T(8,128)S(1)}, u32[]{:S(2)}, u32[]{:S(2)}) %collective-permute-start.3) | collective-permute-done | bytes 32800 | tf_op jit(solution)/shard_map/ppermute | solution.py:286
  28.0 3.1 %collective-permute-start.4 = (f32[1,16,256]{2,1,0:T(8,128)S(1)}, f32[1,16,256]{2,1,0:T(8,128)S(1)}, u32[]{:S(2)}, u32[]{:S(2)}) collective-permute-start(f32[1,16,256]{2,1,0:T(8,128)S(1)} %constant_dynamic-slice_fusion), channel_id=1, source_target_pairs={{0,8},{1,9},{2,10},{3,11},{4,12},{5,13},{6,14},{7,15},{8,0},{9,1},... | collective-permute-start | bytes 49160 | tf_op jit(solution)/shard_map/ppermute | solution.py:286
  31.1 1.7 %collective-permute-done.4 = f32[1,16,256]{2,1,0:T(8,128)S(1)} collective-permute-done((f32[1,16,256]{2,1,0:T(8,128)S(1)}, f32[1,16,256]{2,1,0:T(8,128)S(1)}, u32[]{:S(2)}, u32[]{:S(2)}) %collective-permute-start.4) | collective-permute-done | bytes 16416 | tf_op jit(solution)/shard_map/ppermute | solution.py:286
  32.8 0.6 %add_bitcast_fusion = f32[16,256]{1,0:T(8,128)} fusion(f32[1,16,256]{2,1,0:T(8,128)S(1)} %collective-permute-done.4, f32[2,16,256]{2,1,0:T(8,128)S(1)} %bitcast_add_fusion.2, s32[]{:T(128)S(6)} %select_n.71), kind=kLoop, calls=%fused_computation.6 | loop fusion | flops 4096 | bytes 49156 | tf_op jit(solution)/shard_map/reshape | solution.py:288
  (7 shorter events, 0.1 us)
Async XLA Ops:
  0.0 3.4 %copy-start.3 = (bf16[512,256]{1,0:T(8,128)(2,1)S(1)}, bf16[512,256]{1,0:T(8,128)(2,1)}, u32[]{:S(2)}) copy-start(bf16[512,256]{1,0:T(8,128)(2,1)} %constant.99.clone.refs_4_.refs_5_) | copy-start | bytes 786436
  0.0 3.4 %copy-start.1 = (s32[1,4]{1,0:T(1,128)S(1)}, s32[1,4]{1,0:T(1,128)}, u32[]{:S(2)}) copy-start(s32[1,4]{1,0:T(1,128)} %refs_3_.1) | copy-start | bytes 52
  0.0 3.4 %copy-start = (s32[16,1024]{1,0:T(8,128)S(1)}, s32[16,1024]{1,0:T(8,128)}, u32[]{:S(2)}) copy-start(s32[16,1024]{1,0:T(8,128)} %refs_2_.5) | copy-start | bytes 196612
  0.0 3.4 %copy-start.2 = (bf16[16]{0:T(256)(128)(2,1)S(1)}, bf16[16]{0:T(256)(128)(2,1)}, u32[]{:S(2)}) copy-start(bf16[16]{0:T(256)(128)(2,1)} %param.8) | copy-start | bytes 100
  2.1 11.6 %collective-permute-start = (bf16[1040,256]{1,0:T(8,128)(2,1)}, bf16[1040,256]{1,0:T(8,128)(2,1)S(1)}, u32[]{:S(2)}, u32[]{:S(2)}) collective-permute-start(bf16[1040,256]{1,0:T(8,128)(2,1)} %pack.1), channel_id=1, source_target_pairs={{1,0},{2,1},{3,2},{4,3},{5,4},{6,5},{7,6},{8,7},{9,8},{10,9},{11,1... | collective-permute-start | bytes 1597448 | tf_op jit(solution)/shard_map/ppermute | solution.py:321
  15.7 2.2 %collective-permute-start.1 = (f32[8,16,256]{2,1,0:T(8,128)S(1)}, f32[8,16,256]{2,1,0:T(8,128)S(1)}, u32[]{:S(2)}, u32[]{:S(2)}) collective-permute-start(f32[8,16,256]{2,1,0:T(8,128)S(1)} %dynamic-slice_bitcast_fusion), channel_id=1, source_target_pairs={{0,1},{1,0},{2,3},{3,2},{4,5},{5,4},{6,7},{7,6},{8,9},{9,8},{10,11... | collective-permute-start | bytes 393224 | tf_op jit(solution)/shard_map/ppermute | solution.py:286
  17.9 5.7 %collective-permute-start.2 = (f32[4,16,256]{2,1,0:T(8,128)S(1)}, f32[4,16,256]{2,1,0:T(8,128)S(1)}, u32[]{:S(2)}, u32[]{:S(2)}) collective-permute-start(f32[4,16,256]{2,1,0:T(8,128)S(1)} %dynamic-slice_bitcast_fusion.1), channel_id=1, source_target_pairs={{0,2},{1,3},{2,0},{3,1},{4,6},{5,7},{6,4},{7,5},{8,10},{9,11},{10,... | collective-permute-start | bytes 196616 | tf_op jit(solution)/shard_map/ppermute | solution.py:286
  23.6 4.4 %collective-permute-start.3 = (f32[2,16,256]{2,1,0:T(8,128)S(1)}, f32[2,16,256]{2,1,0:T(8,128)S(1)}, u32[]{:S(2)}, u32[]{:S(2)}) collective-permute-start(f32[2,16,256]{2,1,0:T(8,128)S(1)} %dynamic-slice_bitcast_fusion.2), channel_id=1, source_target_pairs={{0,4},{1,5},{2,6},{3,7},{4,0},{5,1},{6,2},{7,3},{8,12},{9,13},{10,... | collective-permute-start | bytes 98312 | tf_op jit(solution)/shard_map/ppermute | solution.py:286
  28.0 4.8 %collective-permute-start.4 = (f32[1,16,256]{2,1,0:T(8,128)S(1)}, f32[1,16,256]{2,1,0:T(8,128)S(1)}, u32[]{:S(2)}, u32[]{:S(2)}) collective-permute-start(f32[1,16,256]{2,1,0:T(8,128)S(1)} %constant_dynamic-slice_fusion), channel_id=1, source_target_pairs={{0,8},{1,9},{2,10},{3,11},{4,12},{5,13},{6,14},{7,15},{8,0},{9,1},... | collective-permute-start | bytes 49160 | tf_op jit(solution)/shard_map/ppermute | solution.py:286

commit v7 on v5

--- a/solution.py
+++ b/solution.py
@@ -221,7 +221,7 @@
     rows_y, rows_x, scale,
     own, halo_ref, material_ref, occupied_ref, moduli_ref, weights_ref, gram_ref,
     out_ref,
-    image,
+    image, turned, kept,
 ):
     lanes, width = own.shape
     depth = material_ref.shape[0]
@@ -237,21 +237,21 @@
     halo_mask = jnp.where(halo_mod > 0.0, 1.0, 0.0)
     own_c = 0.25 * smooth_plane(halo_mod, rows_y, rows_x) * own_mask
     halo_c = 0.25 * smooth_plane(own_mod, rows_y, rows_x) * halo_mask
-    halo_t = halo_ref[:lanes, :].T
-    halo_on = halo_t * halo_mask[0:1].astype(BF16)
-    own_t = own[...].T
-    own_on = own_t * own_mask[0:1].astype(BF16)
+    turned[0] = halo_ref[:lanes, :].T
+    turned[1] = own[...].T
+    kept[0] = turned[0] * halo_mask[0:1].astype(BF16)
+    kept[1] = turned[1] * own_mask[0:1].astype(BF16)
     for start, low, high in windows(lanes):
         block = slice(start, start + BLOCK)
         first = low - (start - EDGE)
         part = weights_ref[first : first + high - low, :]
-        from_halo = jnp.dot(halo_on[:, low:high], part, preferred_element_type=F32)
-        from_own = jnp.dot(own_on[:, low:high], part, preferred_element_type=F32)
+        from_halo = jnp.dot(kept[0, :, low:high], part, preferred_element_type=F32)
         image[0, :, block] = image_block(
-            own_t[:, block], from_halo, own_mod[:, block], own_c[:, block]
+            turned[1, :, block], from_halo, own_mod[:, block], own_c[:, block]
         )
+        from_own = jnp.dot(kept[1, :, low:high], part, preferred_element_type=F32)
         image[1, :, block] = image_block(
-            halo_t[:, block], from_own, halo_mod[:, block], halo_c[:, block]
+            turned[0, :, block], from_own, halo_mod[:, block], halo_c[:, block]
         )
     total = gram_ref[...]
     total += jnp.dot(image[0], own[...], preferred_element_type=F32)
@@ -342,7 +342,7 @@
         in_specs=[vmem, vmem, vmem, smem, vmem, vmem, vmem],
         out_specs=vmem,
         out_shape=jax.ShapeDtypeStruct((width, width), F32),
-        scratch_shapes=[pltpu.VMEM((2, width, lanes), BF16)],
+        scratch_shapes=[pltpu.VMEM((2, width, lanes), BF16)] * 3,
         compiler_params=pltpu.CompilerParams(vmem_limit_bytes=40 << 20),
         cost_estimate=pl.CostEstimate(
             flops=12 * lanes * width * width, bytes_accessed=4 * lanes * width, transcendentals=0

time: 33.5 us -> 33.6 us (level)
  no operation moved by 1% of the time
where the time goes in v7:
time: 33.6 us; the launch traced here: 33.4 us
  Pallas kernels  14.3 us (43%)
  starting transfers between devices  11.1 us (33%)
  waiting for transfers between devices  7.21 us (21%)
  other arithmetic  0.64 us (2%)
    pallas_call x1, Pallas kernels, local(): pl.pallas_call(lambda *refs: main_kernel(rows_y, rows_x, *refs), in_specs...  10.3 us
    ppermute x4, starting transfers between devices, scatter_sum(): value = keep + lax.ppermute(give, axis, swap)  9.81 us
    ppermute x4, waiting for transfers between devices, scatter_sum(): value = keep + lax.ppermute(give, axis, swap)  7.2 us
    pallas_call x1, Pallas kernels, local(): pl.pallas_call(lambda *refs: edge_kernel(rows_y, rows_x, scale, *refs), i...  2.02 us
    pallas_call x1, Pallas kernels, local(): pl.pallas_call(lambda *refs: pack_kernel(rows_y, rows_x, *refs), in_specs...  1.96 us
    ppermute x1, starting transfers between devices, local(): lax.ppermute(packed, 'bricks', [(i + 1, i) for i in range(owners - 1)])  1.29 us
  transfers between devices with their start and end apart: 5, of which 4 were waited for; matrix products, arithmetic and copies ran while one was open for 0% of the time, Pallas kernels for 31%

profile of v7, /device:TPU:0, one launch (start us, length us, event | category | flops | bytes accessed | tf_op | source)
XLA Modules:
  0.0 33.4 jit_solution(17544388602649970656)
XLA Ops:
  0.0 0.0 copy-start.3
  0.0 0.0 copy-start.1
  0.0 0.0 copy-start
  0.0 0.0 copy-start.2
  0.0 2.0 %pack.1 = bf16[1040,256]{1,0:T(8,128)(2,1)} custom-call(bf16[16,1024,256]{2,1,0:T(8,128)(2,1)} %bitcast.24, s32[16,1024]{1,0:T(8,128)} %refs_2_.5, s32[1,4]{1,0:T(1,128)} %refs_3_.1, bf16[1,16]{1,0:T(2,128)(2,1)} %bitcast.21), custom_call_target="tpu_custom_call" | custom-call | tf_op jit(solution)/shard_map/pack/pallas_call | solution.py:291
  2.0 1.3 %collective-permute-start = (bf16[1040,256]{1,0:T(8,128)(2,1)}, bf16[1040,256]{1,0:T(8,128)(2,1)S(1)}, u32[]{:S(2)}, u32[]{:S(2)}) collective-permute-start(bf16[1040,256]{1,0:T(8,128)(2,1)} %pack.1), channel_id=1, source_target_pairs={{1,0},{2,1},{3,2},{4,3},{5,4},{6,5},{7,6},{8,7},{9,8},{10,9},{11,1... | collective-permute-start | bytes 1597448 | tf_op jit(solution)/shard_map/ppermute | solution.py:308
  3.3 0.0 copy-done.3
  3.3 0.0 copy-done.1
  3.3 0.0 copy-done
  3.3 0.0 copy-done.2
  3.3 10.3 %interior.1 = (f32[256,256]{1,0:T(8,128)S(1)}, bf16[1024,256]{1,0:T(8,128)(2,1)S(1)}) custom-call(bf16[16,1024,256]{2,1,0:T(8,128)(2,1)} %bitcast.25, s32[16,1024]{1,0:T(8,128)S(1)} %copy-done, s32[1,4]{1,0:T(1,128)S(1)} %copy-done.1, bf16[1,16]{1,0:T(2,128)(2,1)S(1)} %bitcast.22, bf16[512,256]{1,0:T(8,128)(2,1)S(1)} %copy-done.3), custom_call_target="tpu_custom_call" | custom-call | flops 6442450944 | bytes 8388608 | tf_op jit(solution)/shard_map/interior/pallas_call | solution.py:310
  13.6 0.0 collective-permute-done.refs_1_
  13.6 2.0 %edge.1 = f32[256,256]{1,0:T(8,128)S(1)} custom-call(bf16[1024,256]{1,0:T(8,128)(2,1)S(1)} %get-tuple-element.7.refs_0_, bf16[1040,256]{1,0:T(8,128)(2,1)S(1)} %collective-permute-done.refs_1_, s32[16,1024]{1,0:T(8,128)S(1)} %copy-done, s32[1,4]{1,0:T(1,128)S(1)} %copy-done.1, bf16[1,16]{1,0:T(2,128)(2,1)S(1)} %bitcast.23, bf16[512,256]{1,0:T(8,128)(2,1)S(1)} %copy-done.3, ...), custom_call_target="tpu_custom_call" | custom-call | flops 805306368 | bytes 1048576 | tf_op jit(solution)/shard_map/edge/pallas_call | solution.py:340
  15.7 1.2 %collective-permute-start.1 = (f32[8,16,256]{2,1,0:T(8,128)S(1)}, f32[8,16,256]{2,1,0:T(8,128)S(1)}, u32[]{:S(2)}, u32[]{:S(2)}) collective-permute-start(f32[8,16,256]{2,1,0:T(8,128)S(1)} %dynamic-slice_bitcast_fusion), channel_id=1, source_target_pairs={{0,1},{1,0},{2,3},{3,2},{4,5},{5,4},{6,7},{7,6},{8,9},{9,8},{10,11... | collective-permute-start | bytes 393224 | tf_op jit(solution)/shard_map/ppermute | solution.py:273
  16.9 1.0 %collective-permute-done.1 = f32[8,16,256]{2,1,0:T(8,128)S(1)} collective-permute-done((f32[8,16,256]{2,1,0:T(8,128)S(1)}, f32[8,16,256]{2,1,0:T(8,128)S(1)}, u32[]{:S(2)}, u32[]{:S(2)}) %collective-permute-start.1) | collective-permute-done | bytes 131104 | tf_op jit(solution)/shard_map/ppermute | solution.py:273
  17.9 3.1 %collective-permute-start.2 = (f32[4,16,256]{2,1,0:T(8,128)S(1)}, f32[4,16,256]{2,1,0:T(8,128)S(1)}, u32[]{:S(2)}, u32[]{:S(2)}) collective-permute-start(f32[4,16,256]{2,1,0:T(8,128)S(1)} %dynamic-slice_bitcast_fusion.1), channel_id=1, source_target_pairs={{0,2},{1,3},{2,0},{3,1},{4,6},{5,7},{6,4},{7,5},{8,10},{9,11},{10,... | collective-permute-start | bytes 196616 | tf_op jit(solution)/shard_map/ppermute | solution.py:273
  21.0 2.6 %collective-permute-done.2 = f32[4,16,256]{2,1,0:T(8,128)S(1)} collective-permute-done((f32[4,16,256]{2,1,0:T(8,128)S(1)}, f32[4,16,256]{2,1,0:T(8,128)S(1)}, u32[]{:S(2)}, u32[]{:S(2)}) %collective-permute-start.2) | collective-permute-done | bytes 65568 | tf_op jit(solution)/shard_map/ppermute | solution.py:273
  23.6 2.5 %collective-permute-start.3 = (f32[2,16,256]{2,1,0:T(8,128)S(1)}, f32[2,16,256]{2,1,0:T(8,128)S(1)}, u32[]{:S(2)}, u32[]{:S(2)}) collective-permute-start(f32[2,16,256]{2,1,0:T(8,128)S(1)} %dynamic-slice_bitcast_fusion.2), channel_id=1, source_target_pairs={{0,4},{1,5},{2,6},{3,7},{4,0},{5,1},{6,2},{7,3},{8,12},{9,13},{10,... | collective-permute-start | bytes 98312 | tf_op jit(solution)/shard_map/ppermute | solution.py:273
  26.1 1.9 %collective-permute-done.3 = f32[2,16,256]{2,1,0:T(8,128)S(1)} collective-permute-done((f32[2,16,256]{2,1,0:T(8,128)S(1)}, f32[2,16,256]{2,1,0:T(8,128)S(1)}, u32[]{:S(2)}, u32[]{:S(2)}) %collective-permute-start.3) | collective-permute-done | bytes 32800 | tf_op jit(solution)/shard_map/ppermute | solution.py:273
  28.0 3.1 %collective-permute-start.4 = (f32[1,16,256]{2,1,0:T(8,128)S(1)}, f32[1,16,256]{2,1,0:T(8,128)S(1)}, u32[]{:S(2)}, u32[]{:S(2)}) collective-permute-start(f32[1,16,256]{2,1,0:T(8,128)S(1)} %constant_dynamic-slice_fusion), channel_id=1, source_target_pairs={{0,8},{1,9},{2,10},{3,11},{4,12},{5,13},{6,14},{7,15},{8,0},{9,1},... | collective-permute-start | bytes 49160 | tf_op jit(solution)/shard_map/ppermute | solution.py:273
  31.1 1.7 %collective-permute-done.4 = f32[1,16,256]{2,1,0:T(8,128)S(1)} collective-permute-done((f32[1,16,256]{2,1,0:T(8,128)S(1)}, f32[1,16,256]{2,1,0:T(8,128)S(1)}, u32[]{:S(2)}, u32[]{:S(2)}) %collective-permute-start.4) | collective-permute-done | bytes 16416 | tf_op jit(solution)/shard_map/ppermute | solution.py:273
  32.8 0.6 %add_bitcast_fusion = f32[16,256]{1,0:T(8,128)} fusion(f32[1,16,256]{2,1,0:T(8,128)S(1)} %collective-permute-done.4, f32[2,16,256]{2,1,0:T(8,128)S(1)} %bitcast_add_fusion.2, s32[]{:T(128)S(6)} %select_n.71), kind=kLoop, calls=%fused_computation.6 | loop fusion | flops 4096 | bytes 49156 | tf_op jit(solution)/shard_map/reshape | solution.py:275
  (7 shorter events, 0.1 us)
Async XLA Ops:
  0.0 3.3 %copy-start.3 = (bf16[512,256]{1,0:T(8,128)(2,1)S(1)}, bf16[512,256]{1,0:T(8,128)(2,1)}, u32[]{:S(2)}) copy-start(bf16[512,256]{1,0:T(8,128)(2,1)} %constant.99.clone.refs_4_.refs_5_) | copy-start | bytes 786436
  0.0 3.3 %copy-start.1 = (s32[1,4]{1,0:T(1,128)S(1)}, s32[1,4]{1,0:T(1,128)}, u32[]{:S(2)}) copy-start(s32[1,4]{1,0:T(1,128)} %refs_3_.1) | copy-start | bytes 52
  0.0 3.3 %copy-start = (s32[16,1024]{1,0:T(8,128)S(1)}, s32[16,1024]{1,0:T(8,128)}, u32[]{:S(2)}) copy-start(s32[16,1024]{1,0:T(8,128)} %refs_2_.5) | copy-start | bytes 196612
  0.0 3.3 %copy-start.2 = (bf16[16]{0:T(256)(128)(2,1)S(1)}, bf16[16]{0:T(256)(128)(2,1)}, u32[]{:S(2)}) copy-start(bf16[16]{0:T(256)(128)(2,1)} %param.8) | copy-start | bytes 100
  2.0 11.6 %collective-permute-start = (bf16[1040,256]{1,0:T(8,128)(2,1)}, bf16[1040,256]{1,0:T(8,128)(2,1)S(1)}, u32[]{:S(2)}, u32[]{:S(2)}) collective-permute-start(bf16[1040,256]{1,0:T(8,128)(2,1)} %pack.1), channel_id=1, source_target_pairs={{1,0},{2,1},{3,2},{4,3},{5,4},{6,5},{7,6},{8,7},{9,8},{10,9},{11,1... | collective-permute-start | bytes 1597448 | tf_op jit(solution)/shard_map/ppermute | solution.py:308
  15.7 2.2 %collective-permute-start.1 = (f32[8,16,256]{2,1,0:T(8,128)S(1)}, f32[8,16,256]{2,1,0:T(8,128)S(1)}, u32[]{:S(2)}, u32[]{:S(2)}) collective-permute-start(f32[8,16,256]{2,1,0:T(8,128)S(1)} %dynamic-slice_bitcast_fusion), channel_id=1, source_target_pairs={{0,1},{1,0},{2,3},{3,2},{4,5},{5,4},{6,7},{7,6},{8,9},{9,8},{10,11... | collective-permute-start | bytes 393224 | tf_op jit(solution)/shard_map/ppermute | solution.py:273
  17.9 5.7 %collective-permute-start.2 = (f32[4,16,256]{2,1,0:T(8,128)S(1)}, f32[4,16,256]{2,1,0:T(8,128)S(1)}, u32[]{:S(2)}, u32[]{:S(2)}) collective-permute-start(f32[4,16,256]{2,1,0:T(8,128)S(1)} %dynamic-slice_bitcast_fusion.1), channel_id=1, source_target_pairs={{0,2},{1,3},{2,0},{3,1},{4,6},{5,7},{6,4},{7,5},{8,10},{9,11},{10,... | collective-permute-start | bytes 196616 | tf_op jit(solution)/shard_map/ppermute | solution.py:273
  23.6 4.4 %collective-permute-start.3 = (f32[2,16,256]{2,1,0:T(8,128)S(1)}, f32[2,16,256]{2,1,0:T(8,128)S(1)}, u32[]{:S(2)}, u32[]{:S(2)}) collective-permute-start(f32[2,16,256]{2,1,0:T(8,128)S(1)} %dynamic-slice_bitcast_fusion.2), channel_id=1, source_target_pairs={{0,4},{1,5},{2,6},{3,7},{4,0},{5,1},{6,2},{7,3},{8,12},{9,13},{10,... | collective-permute-start | bytes 98312 | tf_op jit(solution)/shard_map/ppermute | solution.py:273
  28.0 4.8 %collective-permute-start.4 = (f32[1,16,256]{2,1,0:T(8,128)S(1)}, f32[1,16,256]{2,1,0:T(8,128)S(1)}, u32[]{:S(2)}, u32[]{:S(2)}) collective-permute-start(f32[1,16,256]{2,1,0:T(8,128)S(1)} %constant_dynamic-slice_fusion), channel_id=1, source_target_pairs={{0,8},{1,9},{2,10},{3,11},{4,12},{5,13},{6,14},{7,15},{8,0},{9,1},... | collective-permute-start | bytes 49160 | tf_op jit(solution)/shard_map/ppermute | solution.py:273
